TPU v7x, 256 devices: a whole 4x4x8 slice. The times are simulated.
256 devices in a mesh: row: 32 (over z, x_lo, core), col: 8 (over y, x_hi).
Axes of the slice: x: 4 (x_hi: 2, x_lo: 2; x = x_hi * 2 + x_lo), y: 4, z: 8, core: 2. Of those that a mesh axis runs over, the one named last changes fastest.
Arguments:
- samples: float32 [4194304], P(('row', 'col')), may hold values from -6 to 6
- stem_weight: float32 [32, 128], replicated, may hold values from -1 to 1
- in_weight: float32 [128, 384], replicated, may hold values from -0.5 to 0.5
- filter_param: float32 [262144, 128], P(('row', 'col')), may hold values from -6 to 6
- out_weight: float32 [128, 128], replicated, may hold values from -0.5 to 0.5
- cotangent: float32 [262144, 128], P(('row', 'col')), may hold values from -6 to 6
Outputs:
- layer_out: float32 [262144, 128], P(('row', 'col'))
- filter_grad: float32 [262144, 128], P(('row', 'col'))
- stem_grad: float32 [32, 128], replicated
- in_grad: float32 [128, 384], replicated
- out_grad: float32 [128, 128], replicated
All inputs are finite; a program needn't handle non-finite values.
Results may differ from a plain program's by a relative error of at most 0.0008.
Values sent between devices are 32-bit elements; how exact they have to be, the bound alone decides.
A program may use at most 128 MiB of HBM per device.

v0:
```python
import math

import jax
import jax.numpy as jnp
from jax import lax
from jax.sharding import PartitionSpec as P

INNER = 1024
STRIDE = 16


HIGHEST_PRECISION = lax.Precision.HIGHEST
EPSILON = 1e-05


def from_behind(value, axis, steps):
    count = lax.axis_size(axis)
    leading, last = (max(0, -steps), min(count, count - steps))
    return lax.ppermute(value, axis, [(source, source + steps) for source in range(leading, last)])


def matmul(left, right):
    return jnp.dot(left, right, preferred_element_type=jnp.float32, precision=HIGHEST_PRECISION)


def contract_rows(left, right):
    return jnp.einsum(
        "tc,td->cd", left, right, preferred_element_type=jnp.float32, precision=HIGHEST_PRECISION
    )


def normalize(stem_out):
    return stem_out * lax.rsqrt(jnp.mean(stem_out * stem_out, axis=1, keepdims=True) + EPSILON)


def dft_tables(length):
    index = lax.iota(jnp.int32, length)
    product = index[:, None] * index[None, :] % length
    angle = product.astype(jnp.float32) * (-2.0 * math.pi / length)
    cosine = jnp.cos(angle)
    sine = jnp.sin(angle)
    return (cosine, sine, cosine + sine)


def outer_apply(table, data):
    return jnp.einsum(
        "ka,abc->kbc", table, data, preferred_element_type=jnp.float32, precision=HIGHEST_PRECISION
    )


def inner_apply(table, data):
    return jnp.einsum(
        "kb,abc->akc", table, data, preferred_element_type=jnp.float32, precision=HIGHEST_PRECISION
    )


def complex_apply(apply, tables, real_part, imaginary):
    first = apply(tables[0], real_part)
    second = apply(tables[1], imaginary)
    third = apply(tables[2], real_part + imaginary)
    return (first - second, third - first - second)


def conjugate_apply(apply, tables, real_part, imaginary):
    result_real, result_imaginary = complex_apply(apply, tables, real_part, -imaginary)
    return (result_real, -result_imaginary)


def rotate(real_part, imaginary, angle):
    cosine = jnp.cos(angle)
    sine = jnp.sin(angle)
    return (real_part * cosine - imaginary * sine, real_part * sine + imaginary * cosine)


def body(samples, stem_weight, in_weight, filter_param, out_weight, cotangent):
    frames_dev, channels = filter_param.shape
    n_row = lax.axis_size("row")
    n_col = lax.axis_size("col")
    devices = n_row * n_col
    total_frames = frames_dev * devices
    blocks_local = frames_dev // INNER
    columns_local = INNER // devices
    outer_length = blocks_local * devices
    device_index = lax.axis_index("row") * n_col + lax.axis_index("col")
    global_scale = 1.0 / math.sqrt(total_frames)
    inverse_scale = 1.0 / total_frames

    def spread_form(data):
        return data.reshape(1, 1, blocks_local, n_row, n_col, columns_local, data.shape[-1])

    def column_form(data):
        return data.reshape(outer_length, columns_local, data.shape[-1])

    def collect_form(data):
        return data.reshape(n_row, n_col, blocks_local, 1, 1, columns_local, data.shape[-1])

    def spectral_form(data):
        return data.reshape(blocks_local, INNER, data.shape[-1])

    outer_tables = dft_tables(outer_length)
    inner_tables = dft_tables(INNER)
    outer_index = lax.iota(jnp.int32, outer_length)
    column_index = device_index * columns_local + lax.iota(jnp.int32, columns_local)
    forward_angle = (
        (outer_index[:, None] * column_index[None, :] % total_frames).astype(jnp.float32)
        * (-2.0 * math.pi / total_frames)
    )[:, :, None]
    block_index = device_index * blocks_local + lax.iota(jnp.int32, blocks_local)
    inner_index = lax.iota(jnp.int32, INNER)
    inverse_angle = (
        (block_index[:, None] * inner_index[None, :] % total_frames).astype(jnp.float32)
        * (2.0 * math.pi / total_frames)
    )[:, :, None]

    def first_section(data):
        columns = column_form(data)
        return rotate(
            outer_apply(outer_tables[0], columns),
            outer_apply(outer_tables[1], columns),
            forward_angle,
        )

    def inverse_first(real_part, imaginary):
        turned_real, turned_imaginary = conjugate_apply(
            inner_apply, inner_tables, real_part, imaginary
        )
        return rotate(turned_real, turned_imaginary, inverse_angle)

    def inverse_real(real_part, imaginary):
        return (
            outer_apply(outer_tables[0], real_part) + outer_apply(outer_tables[1], imaginary)
        ) * inverse_scale

    own_samples = samples.reshape(frames_dev, STRIDE)
    edge_samples = from_behind(samples[:STRIDE], ("row", "col"), -1)
    following = jnp.concatenate([own_samples[1:], edge_samples[None, :]], axis=0)
    windows = jnp.concatenate([own_samples, following], axis=1)
    stem_out = matmul(windows, stem_weight)
    normed, norm_back = jax.vjp(normalize, stem_out)
    projected = matmul(normed, in_weight)
    query_part = projected[:, :channels]
    key_part = projected[:, channels : 2 * channels]
    value_part = projected[:, 2 * channels :]
    mixed_in = key_part * value_part
    filter_time = filter_param * global_scale
    gated_grad = jnp.einsum(
        "tc,dc->td",
        cotangent,
        out_weight,
        preferred_element_type=jnp.float32,
        precision=HIGHEST_PRECISION,
    )
    conv_grad = gated_grad * query_part
    spread = (
        lax.all_to_all(
            lax.all_to_all(spread_form(mixed_in), "row", split_axis=3, concat_axis=0, tiled=True),
            "col",
            split_axis=4,
            concat_axis=1,
            tiled=True,
        ),
        lax.all_to_all(
            lax.all_to_all(
                spread_form(filter_time), "row", split_axis=3, concat_axis=0, tiled=True
            ),
            "col",
            split_axis=4,
            concat_axis=1,
            tiled=True,
        ),
    )
    mixed_cols = first_section(spread[0])
    filter_cols = first_section(spread[1])
    collected = (
        lax.all_to_all(
            lax.all_to_all(
                collect_form(mixed_cols[0]), "row", split_axis=0, concat_axis=3, tiled=True
            ),
            "col",
            split_axis=1,
            concat_axis=4,
            tiled=True,
        ),
        lax.all_to_all(
            lax.all_to_all(
                collect_form(mixed_cols[1]), "row", split_axis=0, concat_axis=3, tiled=True
            ),
            "col",
            split_axis=1,
            concat_axis=4,
            tiled=True,
        ),
        lax.all_to_all(
            lax.all_to_all(
                collect_form(filter_cols[0]), "row", split_axis=0, concat_axis=3, tiled=True
            ),
            "col",
            split_axis=1,
            concat_axis=4,
            tiled=True,
        ),
        lax.all_to_all(
            lax.all_to_all(
                collect_form(filter_cols[1]), "row", split_axis=0, concat_axis=3, tiled=True
            ),
            "col",
            split_axis=1,
            concat_axis=4,
            tiled=True,
        ),
    )
    mixed_spec = complex_apply(
        inner_apply, inner_tables, spectral_form(collected[0]), spectral_form(collected[1])
    )
    filter_spec = complex_apply(
        inner_apply, inner_tables, spectral_form(collected[2]), spectral_form(collected[3])
    )
    product_real = mixed_spec[0] * filter_spec[0] - mixed_spec[1] * filter_spec[1]
    product_imaginary = mixed_spec[0] * filter_spec[1] + mixed_spec[1] * filter_spec[0]
    turned = inverse_first(product_real, product_imaginary)
    spread_back = (
        lax.all_to_all(
            lax.all_to_all(spread_form(turned[0]), "row", split_axis=3, concat_axis=0, tiled=True),
            "col",
            split_axis=4,
            concat_axis=1,
            tiled=True,
        ),
        lax.all_to_all(
            lax.all_to_all(spread_form(turned[1]), "row", split_axis=3, concat_axis=0, tiled=True),
            "col",
            split_axis=4,
            concat_axis=1,
            tiled=True,
        ),
    )
    conv_cols = inverse_real(column_form(spread_back[0]), column_form(spread_back[1]))
    long_conv = lax.all_to_all(
        lax.all_to_all(collect_form(conv_cols), "row", split_axis=0, concat_axis=3, tiled=True),
        "col",
        split_axis=1,
        concat_axis=4,
        tiled=True,
    ).reshape(frames_dev, channels)
    gated = query_part * long_conv
    local = contract_rows(gated, cotangent)
    grad_spread = lax.all_to_all(
        lax.all_to_all(spread_form(conv_grad), "row", split_axis=3, concat_axis=0, tiled=True),
        "col",
        split_axis=4,
        concat_axis=1,
        tiled=True,
    )
    grad_cols = first_section(grad_spread)
    grad_collected = (
        lax.all_to_all(
            lax.all_to_all(
                collect_form(grad_cols[0]), "row", split_axis=0, concat_axis=3, tiled=True
            ),
            "col",
            split_axis=1,
            concat_axis=4,
            tiled=True,
        ),
        lax.all_to_all(
            lax.all_to_all(
                collect_form(grad_cols[1]), "row", split_axis=0, concat_axis=3, tiled=True
            ),
            "col",
            split_axis=1,
            concat_axis=4,
            tiled=True,
        ),
    )
    grad_spec = complex_apply(
        inner_apply,
        inner_tables,
        spectral_form(grad_collected[0]),
        spectral_form(grad_collected[1]),
    )
    input_real = filter_spec[0] * grad_spec[0] + filter_spec[1] * grad_spec[1]
    input_imaginary = filter_spec[0] * grad_spec[1] - filter_spec[1] * grad_spec[0]
    weight_real = mixed_spec[0] * grad_spec[0] + mixed_spec[1] * grad_spec[1]
    weight_imaginary = mixed_spec[0] * grad_spec[1] - mixed_spec[1] * grad_spec[0]
    input_turned = inverse_first(input_real, input_imaginary)
    weight_turned = inverse_first(weight_real, weight_imaginary)
    pair_back = (
        lax.all_to_all(
            lax.all_to_all(
                spread_form(jnp.concatenate([input_turned[0], weight_turned[0]], axis=-1)),
                "row",
                split_axis=3,
                concat_axis=0,
                tiled=True,
            ),
            "col",
            split_axis=4,
            concat_axis=1,
            tiled=True,
        ),
        lax.all_to_all(
            lax.all_to_all(
                spread_form(jnp.concatenate([input_turned[1], weight_turned[1]], axis=-1)),
                "row",
                split_axis=3,
                concat_axis=0,
                tiled=True,
            ),
            "col",
            split_axis=4,
            concat_axis=1,
            tiled=True,
        ),
    )
    real_part = column_form(pair_back[0])
    imaginary = column_form(pair_back[1])
    first_cols = inverse_real(real_part[..., :channels], imaginary[..., :channels])
    second_cols = inverse_real(real_part[..., channels:], imaginary[..., channels:])
    both_back = (
        lax.all_to_all(
            lax.all_to_all(
                collect_form(first_cols), "row", split_axis=0, concat_axis=3, tiled=True
            ),
            "col",
            split_axis=1,
            concat_axis=4,
            tiled=True,
        ),
        lax.all_to_all(
            lax.all_to_all(
                collect_form(second_cols), "row", split_axis=0, concat_axis=3, tiled=True
            ),
            "col",
            split_axis=1,
            concat_axis=4,
            tiled=True,
        ),
    )
    input_grad = both_back[0].reshape(frames_dev, channels)
    filter_grad = both_back[1].reshape(frames_dev, channels) * global_scale
    layer_out = matmul(gated, out_weight) + stem_out
    query_grad = gated_grad * long_conv
    proj_grad = jnp.concatenate(
        [query_grad, input_grad * value_part, input_grad * key_part], axis=1
    )
    in_grad_local = contract_rows(normed, proj_grad)
    normed_grad = jnp.einsum(
        "te,ce->tc",
        proj_grad,
        in_weight,
        preferred_element_type=jnp.float32,
        precision=HIGHEST_PRECISION,
    )
    stem_grad_out = cotangent + norm_back(normed_grad)[0]
    stem_grad_local = contract_rows(windows, stem_grad_out)
    in_grad_sum, stem_grad_sum, out_grad_sum = lax.psum(
        (in_grad_local, stem_grad_local, local), ("row", "col")
    )
    return (
        layer_out,
        filter_grad,
        stem_grad_sum * global_scale,
        in_grad_sum * global_scale,
        out_grad_sum * global_scale,
    )


def solution(mesh):
    in_specs = (P(("row", "col")), P(), P(), P(("row", "col"), None), P(), P(("row", "col"), None))
    out_specs = (P(("row", "col"), None), P(("row", "col"), None), P(), P(), P())
    return jax.shard_map(body, mesh=mesh, in_specs=in_specs, out_specs=out_specs, check_vma=False)
```

profile of v0, /device:TPU:1, one launch (start us, length us, event | category | flops | bytes accessed | tf_op | source)
XLA Modules:
  0.0 1341.7 jit_solution(4507123973428466218)
XLA Ops:
  7.9 8.6 collective-permute-start
  18.4 8.9 all-to-all-start.6
  32.1 11.8 all-to-all-done.6
  44.7 21.9 %all_to_all.438 = f32[1,1,1,32,8,4,128]{6,5,4,2,1,0,3:T(4,128)S(1)} all-to-all(f32[1,1,1,32,8,4,128]{6,5,4,2,1,0,3:T(4,128)} %bitcast.349), channel_id=1, replica_groups=mesh['row'=32,'col'=8] {'row'}, dimensions={3} | all-to-all | bytes 1048576 | tf_op jit(solution)/shard_map/all_to_all | solution.py:248
  66.6 5.5 all-to-all-start
  74.2 14.9 %all-to-all-done = f32[1,1,1,32,8,4,128]{6,5,4,2,1,0,3:T(4,128)} async-done(((f32[1,1,1,32,8,4,128]{6,5,4,2,1,0,3:T(4,128)}), f32[1,1,1,32,8,4,128]{6,5,4,2,1,0,3:T(4,128)}, u32[]{:S(2)}, u32[]{:S(2)}) %all-to-all-start) | async-done | bytes 524320 | tf_op jit(solution)/shard_map/all_to_all | solution.py:156
  96.9 6.8 all-to-all-done.7
  117.3 5.2 all-to-all-start.1
  139.7 8.0 all-to-all-start.22
  149.9 14.9 %all-to-all-done.22 = f32[32,8,1,1,1,4,128]{6,5,1,4,3,2,0:T(4,128)} async-done(((f32[32,8,1,1,1,4,128]{6,5,1,4,3,2,0:T(4,128)}), f32[32,8,1,1,1,4,128]{6,5,1,4,3,2,0:T(4,128)}, u32[]{:S(2)}, u32[]{:S(2)}) %all-to-all-start.22) | async-done | bytes 524320 | tf_op jit(solution)/shard_map/all_to_all | solution.py:266
  164.7 5.5 all-to-all-start.20
  172.5 14.9 %all-to-all-done.20 = f32[32,8,1,1,1,4,128]{6,5,1,4,3,2,0:T(4,128)} async-done(((f32[32,8,1,1,1,4,128]{6,5,1,4,3,2,0:T(4,128)}), f32[32,8,1,1,1,4,128]{6,5,1,4,3,2,0:T(4,128)}, u32[]{:S(2)}, u32[]{:S(2)}) %all-to-all-start.20) | async-done | bytes 524320 | tf_op jit(solution)/shard_map/all_to_all | solution.py:257
  187.3 5.5 all-to-all-start.10
  195.0 14.9 %all-to-all-done.10 = f32[32,8,1,1,1,4,128]{6,5,1,4,3,2,0:T(4,128)} async-done(((f32[32,8,1,1,1,4,128]{6,5,1,4,3,2,0:T(4,128)}), f32[32,8,1,1,1,4,128]{6,5,1,4,3,2,0:T(4,128)}, u32[]{:S(2)}, u32[]{:S(2)}) %all-to-all-start.10) | async-done | bytes 524320 | tf_op jit(solution)/shard_map/all_to_all | solution.py:203
  209.9 5.5 all-to-all-start.8
  217.7 14.9 %all-to-all-done.8 = f32[32,8,1,1,1,4,128]{6,5,1,4,3,2,0:T(4,128)} async-done(((f32[32,8,1,1,1,4,128]{6,5,1,4,3,2,0:T(4,128)}), f32[32,8,1,1,1,4,128]{6,5,1,4,3,2,0:T(4,128)}, u32[]{:S(2)}, u32[]{:S(2)}) %all-to-all-start.8) | async-done | bytes 524320 | tf_op jit(solution)/shard_map/all_to_all | solution.py:194
  232.5 5.5 all-to-all-start.4
  239.2 15.9 %all-to-all-done.4 = f32[32,8,1,1,1,4,128]{6,5,1,4,3,2,0:T(4,128)} async-done(((f32[32,8,1,1,1,4,128]{6,5,1,4,3,2,0:T(4,128)}), f32[32,8,1,1,1,4,128]{6,5,1,4,3,2,0:T(4,128)}, u32[]{:S(2)}, u32[]{:S(2)}) %all-to-all-start.4) | async-done | bytes 524320 | tf_op jit(solution)/shard_map/all_to_all | solution.py:185
  255.1 5.0 all-to-all-start.2
  262.1 15.1 %all-to-all-done.2 = f32[32,8,1,1,1,4,128]{6,5,1,4,3,2,0:T(4,128)S(1)} async-done(((f32[32,8,1,1,1,4,128]{6,5,1,4,3,2,0:T(4,128)}), f32[32,8,1,1,1,4,128]{6,5,1,4,3,2,0:T(4,128)S(1)}, u32[]{:S(2)}, u32[]{:S(2)}) %all-to-all-start.2) | async-done | bytes 524320 | tf_op jit(solution)/shard_map/all_to_all | solution.py:176
  291.3 6.0 all-to-all-start.21
  299.3 20.5 %fusion.72 = f32[1,1024,128]{1,2,0:T(8,128)} fusion(f32[1024,128]{1,0:T(8,128)S(1)} %bitcast.352), kind=kOutput, calls=%fused_computation.41 | convolution fusion | flops 1625292800 | bytes 1048576 | tf_op jit(solution)/shard_map/kb,abc->akc/dot_general | solution.py:52
  319.8 6.6 all-to-all-start.11
  327.4 20.4 %fusion.90 = f32[1,1024,128]{1,2,0:T(8,128)} fusion(f32[1024,128]{1,0:T(8,128)S(1)} %bitcast.354), kind=kOutput, calls=%fused_computation.47 | convolution fusion | flops 1625292800 | bytes 1048576 | tf_op jit(solution)/shard_map/kb,abc->akc/dot_general | solution.py:52
  347.8 6.9 all-to-all-start.9
  356.7 20.5 %fusion.66 = f32[1,1024,128]{1,2,0:T(8,128)} fusion(f32[1024,128]{1,0:T(8,128)S(1)} %bitcast.356), kind=kOutput, calls=%fused_computation.39 | convolution fusion | flops 1625292800 | bytes 1048576 | tf_op jit(solution)/shard_map/kb,abc->akc/dot_general | solution.py:52
  377.2 6.6 all-to-all-start.5
  384.8 20.4 %fusion.84 = f32[1,1024,128]{1,2,0:T(8,128)} fusion(f32[1024,128]{1,0:T(8,128)S(1)} %bitcast.358), kind=kOutput, calls=%fused_computation.45 | convolution fusion | flops 1625292800 | bytes 1048576 | tf_op jit(solution)/shard_map/kb,abc->akc/dot_general | solution.py:52
  405.2 7.1 all-to-all-start.3
  414.3 20.5 %fusion.63 = f32[1,1024,128]{1,2,0:T(8,128)} fusion(f32[1024,128]{1,0:T(8,128)S(1)} %bitcast.361), kind=kOutput, calls=%fused_computation.38 | convolution fusion | flops 1625292800 | bytes 1048576 | tf_op jit(solution)/shard_map/kb,abc->akc/dot_general | solution.py:52
  435.0 20.0 %fusion.81 = f32[1,1024,128]{1,2,0:T(8,128)S(1)} fusion(f32[1024,128]{1,0:T(8,128)S(1)} %bitcast.363), kind=kOutput, calls=%fused_computation.44 | convolution fusion | flops 1625292800 | bytes 1048576 | tf_op jit(solution)/shard_map/kb,abc->akc/dot_general | solution.py:52
  455.1 21.3 %fusion.135 = f32[1,1024,128]{1,2,0:T(8,128)S(1)} fusion(f32[1,1024,128]{1,2,0:T(8,128)S(1)} %copy-done.33, f32[1,1024,128]{1,2,0:T(8,128)S(1)} %copy-done.34, f32[1024,128]{1,0:T(8,128)S(1)} %bitcast.355, f32[1024,128]{1,0:T(8,128)S(1)} %bitcast.353), kind=kOutput, calls=%fused_computation.69 | convolution fusion | flops 1626734592 | bytes 2621440 | tf_op jit(solution)/shard_map/kb,abc->akc/dot_general | solution.py:52
  476.4 21.5 %multiply_add_fusion.3 = (f32[1,1024,128]{1,2,0:T(8,128)S(1)}, f32[1,1024,128]{1,2,0:T(8,128)S(1)}, f32[1,1024,128]{1,2,0:T(8,128)S(1)}, f32[1,1024,128]{1,2,0:T(8,128)S(1)}) fusion(f32[1,1024,128]{1,2,0:T(8,128)S(1)} %fusion.135, f32[1,1024,128]{1,2,0:T(8,128)S(1)} %copy-done.34, f32[1,1024,128]{1,2,0:T(8,128)S(1)} %copy-done.33, ...), kind=kOutput, calls=%fused_computation.128 | convolution fusion | flops 1627389952 | bytes 5767168 | tf_op jit(solution)/shard_map/kb,abc->akc/dot_general | solution.py:52
  498.0 21.8 %multiply_add_fusion.2 = (f32[1,1024,128]{1,2,0:T(8,128)S(1)}, f32[1,1024,128]{1,2,0:T(8,128)S(1)}, f32[1,1024,128]{1,2,0:T(8,128)S(1)}, f32[1,1024,128]{1,2,0:T(8,128)S(1)}) fusion(f32[1,1024,128]{1,2,0:T(8,128)S(1)} %fusion.135, f32[1,1024,128]{1,2,0:T(8,128)S(1)} %get-tuple-element.28, f32[1,1024,128]{1,2,0:T(8,128)S(1)} %fusion.81, ...), kind=kOutput, calls=%fused_computation.124 | convolution fusion | flops 1627783168 | bytes 6291456 | tf_op jit(solution)/shard_map/kb,abc->akc/dot_general | solution.py:52
  520.2 20.2 %fusion.78 = f32[1,1024,128]{1,2,0:T(8,128)S(1)} fusion(f32[1,1024,128]{1,2,0:T(8,128)S(1)} %get-tuple-element.51), kind=kOutput, calls=%fused_computation.43 | convolution fusion | flops 1625292800 | bytes 1048576 | tf_op jit(solution)/shard_map/kb,abc->akc/dot_general | solution.py:52
  540.4 19.9 %fusion.96 = f32[1,1024,128]{1,2,0:T(8,128)S(1)} fusion(f32[1,1024,128]{1,2,0:T(8,128)S(1)} %get-tuple-element.30), kind=kOutput, calls=%fused_computation.49 | convolution fusion | flops 1625292800 | bytes 1048576 | tf_op jit(solution)/shard_map/kb,abc->akc/dot_general | solution.py:52
  560.4 20.3 %fusion.69 = f32[1,1024,128]{1,2,0:T(8,128)S(1)} fusion(f32[1,1024,128]{1,2,0:T(8,128)S(1)} %get-tuple-element.35), kind=kOutput, calls=%fused_computation.40 | convolution fusion | flops 1625292800 | bytes 1048576 | tf_op jit(solution)/shard_map/kb,abc->akc/dot_general | solution.py:52
  580.6 19.9 %fusion.87 = f32[1,1024,128]{1,2,0:T(8,128)S(1)} fusion(f32[1,1024,128]{1,2,0:T(8,128)S(1)} %get-tuple-element.34), kind=kOutput, calls=%fused_computation.46 | convolution fusion | flops 1625292800 | bytes 1048576 | tf_op jit(solution)/shard_map/kb,abc->akc/dot_general | solution.py:52
  600.6 20.5 %fusion.75 = f32[1,1024,128]{1,2,0:T(8,128)S(1)} fusion(f32[1,1024,128]{1,2,0:T(8,128)S(1)} %get-tuple-element.50), kind=kOutput, calls=%fused_computation.42 | convolution fusion | flops 1625292800 | bytes 1048576 | tf_op jit(solution)/shard_map/kb,abc->akc/dot_general | solution.py:52
  621.0 19.9 %fusion.93 = f32[1,1024,128]{1,2,0:T(8,128)S(1)} fusion(f32[1,1024,128]{1,2,0:T(8,128)S(1)} %get-tuple-element.27), kind=kOutput, calls=%fused_computation.48 | convolution fusion | flops 1625292800 | bytes 1048576 | tf_op jit(solution)/shard_map/kb,abc->akc/dot_general | solution.py:52
  641.0 21.4 %fusion.147 = f32[1,1024,128]{1,2,0:T(8,128)S(1)} fusion(f32[1,1024,128]{1,2,0:T(8,128)S(1)} %fusion.78, f32[1,1024,128]{1,2,0:T(8,128)S(1)} %fusion.96, f32[1,1024,128]{1,2,0:T(8,128)S(1)} %get-tuple-element.30, f32[1,1024,128]{1,2,0:T(8,128)S(1)} %get-tuple-element.51), kind=kOutput, calls=%fused_computation.73 | convolution fusion | flops 1626865664 | bytes 2621440 | tf_op jit(solution)/shard_map/kb,abc->akc/dot_general | solution.py:52
  662.4 21.4 %fusion.132 = f32[1,1024,128]{1,2,0:T(8,128)S(1)} fusion(f32[1,1024,128]{1,2,0:T(8,128)S(1)} %fusion.69, f32[1,1024,128]{1,2,0:T(8,128)S(1)} %fusion.87, f32[1,1024,128]{1,2,0:T(8,128)S(1)} %get-tuple-element.34, f32[1,1024,128]{1,2,0:T(8,128)S(1)} %get-tuple-element.35), kind=kOutput, calls=%fused_computation.68 | convolution fusion | flops 1626865664 | bytes 2621440 | tf_op jit(solution)/shard_map/kb,abc->akc/dot_general | solution.py:52
  683.8 22.6 %multiply_add_fusion.1 = (f32[1,1024,128]{1,2,0:T(8,128)}, f32[1,1024,128]{1,2,0:T(8,128)}, f32[1,1024,128]{1,2,0:T(8,128)S(1)}, f32[1,1024,128]{1,2,0:T(8,128)}...) fusion(f32[1024]{0:T(1024)S(1)} %copy-done.30, f32[1024]{0:T(1024)S(1)} %copy-done.31, ...), kind=kOutput, calls=%fused_computation.120 | convolution fusion | flops 1629618176 | bytes 8396800 | tf_op jit(solution)/shard_map/kb,abc->akc/dot_general | solution.py:52
  707.4 7.9 all-to-all-start.12
  717.4 15.0 %all-to-all-done.12 = f32[1,1,1,32,8,4,128]{6,5,4,2,1,0,3:T(4,128)S(1)} async-done(((f32[1,1,1,32,8,4,128]{6,5,4,2,1,0,3:T(4,128)}), f32[1,1,1,32,8,4,128]{6,5,4,2,1,0,3:T(4,128)S(1)}, u32[]{:S(2)}, u32[]{:S(2)}) %all-to-all-start.12) | async-done | bytes 524320 | tf_op jit(solution)/shard_map/all_to_all | solution.py:223
  732.4 5.5 all-to-all-start.14
  738.8 16.2 %all-to-all-done.14 = f32[1,1,1,32,8,4,128]{6,5,4,2,1,0,3:T(4,128)} async-done(((f32[1,1,1,32,8,4,128]{6,5,4,2,1,0,3:T(4,128)}), f32[1,1,1,32,8,4,128]{6,5,4,2,1,0,3:T(4,128)}, u32[]{:S(2)}, u32[]{:S(2)}) %all-to-all-start.14) | async-done | bytes 524320 | tf_op jit(solution)/shard_map/all_to_all | solution.py:230
  755.0 6.9 all-to-all-start.13
  763.8 7.8 all-to-all-done.13
  785.1 8.1 all-to-all-start.26
  799.1 22.1 %all-to-all-done.26 = f32[1,1,1,32,8,4,256]{6,0,5,4,2,1,3:T(1,128)} async-done(((f32[1,1,1,32,8,4,256]{6,0,5,4,2,1,3:T(1,128)}), f32[1,1,1,32,8,4,256]{6,0,5,4,2,1,3:T(1,128)}, u32[]{:S(2)}, u32[]{:S(2)}) %all-to-all-start.26) | async-done | bytes 1048608 | tf_op jit(solution)/shard_map/all_to_all | solution.py:302
  821.2 6.2 all-to-all-start.24
  833.3 21.9 %all-to-all-done.24 = f32[1,1,1,32,8,4,256]{6,0,5,4,2,1,3:T(1,128)} async-done(((f32[1,1,1,32,8,4,256]{6,0,5,4,2,1,3:T(1,128)}), f32[1,1,1,32,8,4,256]{6,0,5,4,2,1,3:T(1,128)}, u32[]{:S(2)}, u32[]{:S(2)}) %all-to-all-start.24) | async-done | bytes 1048608 | tf_op jit(solution)/shard_map/all_to_all | solution.py:289
  855.2 5.1 all-to-all-start.16
  863.3 14.0 %all-to-all-done.16 = f32[32,8,1,1,1,4,128]{6,5,1,4,3,2,0:T(4,128)S(1)} async-done(((f32[32,8,1,1,1,4,128]{6,5,1,4,3,2,0:T(4,128)}), f32[32,8,1,1,1,4,128]{6,5,1,4,3,2,0:T(4,128)S(1)}, u32[]{:S(2)}, u32[]{:S(2)}) %all-to-all-start.16) | async-done | bytes 524320 | tf_op jit(solution)/shard_map/all_to_all | solution.py:239
  884.6 12.7 all-to-all-done.27
  902.4 13.9 %all-to-all-done.25 = f32[32,1,1,1,8,4,256]{6,1,5,3,2,0,4:T(1,128)} async-done(((f32[32,1,1,1,8,4,256]{6,1,5,3,2,0,4:T(1,128)}), f32[32,1,1,1,8,4,256]{6,1,5,3,2,0,4:T(1,128)}, u32[]{:S(2)}, u32[]{:S(2)}) %all-to-all-start.25) | async-done | bytes 1048608 | tf_op jit(solution)/shard_map/all_to_all | solution.py:288
  929.0 10.2 all-to-all-start.30
  945.4 10.2 all-to-all-done.30
  955.6 5.5 all-to-all-start.28
  967.2 11.0 all-to-all-done.28
  978.2 5.1 all-to-all-start.31
  1002.2 77.2 %psum.21 = f32[32,128]{1,0:T(8,128)S(1)} all-reduce(f32[32,128]{1,0:T(8,128)S(1)} %fusion.153), channel_id=1, replica_groups=mesh['row'=32,'col'=8] {'row','col'}, use_global_device_ids=true, to_apply=%region_2.3 | all-reduce | flops 4096 | bytes 32768 | tf_op jit(solution)/shard_map/psum | solution.py:356
  1084.0 247.5 %all-reduce.3.cloned.1.call-done = (f32[128,384]{1,0:T(8,128)}, f32[128,128]{1,0:T(8,128)}) async-done(((f32[128,384]{1,0:T(8,128)}, f32[128,128]{1,0:T(8,128)}), (f32[128,384]{1,0:T(8,128)}, f32[128,128]{1,0:T(8,128)})) %all-reduce.3.cloned.1.call-update) | async-done | bytes 262160 | tf_op jit(solution)/shard_map/psum | solution.py:356
  (182 shorter events, 181.0 us)
Async XLA Ops:
  7.2 21.7 %copy-start = (f32[128,384]{1,0:T(8,128)S(1)}, f32[128,384]{1,0:T(8,128)}, u32[]{:S(2)}) copy-start(f32[128,384]{1,0:T(8,128)} %param.8) | copy-start | bytes 589828
  7.9 19.4 %copy-start.27 = (f32[16384]{0:T(1024)S(1)}, f32[16384]{0:T(1024)}, u32[]{:S(2)}) copy-start(f32[16384]{0:T(1024)} %param.6) | copy-start | bytes 196612
  7.9 20.3 %collective-permute-start = (f32[16]{0:T(128)S(1)}, f32[16]{0:T(128)S(1)}, u32[]{:S(2)}, u32[]{:S(2)}) collective-permute-start(f32[16]{0:T(128)S(1)} %slice.40), channel_id=1, source_target_pairs={{1,0},{2,1},{3,2},{4,3},{5,4},{6,5},{7,6},{8,7},{9,8},{10,9},{11,1... | collective-permute-start | bytes 200 | tf_op jit(solution)/shard_map/ppermute | solution.py:19
  18.4 9.8 copy-start.29
  18.4 25.5 %all-to-all-start.6 = ((f32[1,1,1,32,8,4,128]{6,4,5,2,1,0,3:T(8,128)}), f32[1,1,1,32,8,4,128]{6,4,5,2,1,0,3:T(8,128)S(1)}, u32[]{:S(2)}, u32[]{:S(2)}) async-start(f32[1,1,1,32,8,4,128]{6,4,5,2,1,0,3:T(8,128)} %copy.115), calls=%async_computation.6 | async-start | bytes 1048576 | tf_op jit(solution)/shard_map/all_to_all | solution.py:163
  28.1 2.2 copy-start.1
  28.2 2.2 copy-start.28
  66.6 22.6 %all-to-all-start = ((f32[1,1,1,32,8,4,128]{6,5,4,2,1,0,3:T(4,128)}), f32[1,1,1,32,8,4,128]{6,5,4,2,1,0,3:T(4,128)}, u32[]{:S(2)}, u32[]{:S(2)}) async-start(f32[1,1,1,32,8,4,128]{6,5,4,2,1,0,3:T(4,128)} %bitcast.348), calls=%async_computation | async-start | bytes 1048576 | tf_op jit(solution)/shard_map/all_to_all | solution.py:156
  89.2 14.5 %all-to-all-start.7 = ((f32[32,1,1,1,8,4,128]{6,0,5,3,2,1,4:T(8,128)}), f32[32,1,1,1,8,4,128]{6,0,5,3,2,1,4:T(8,128)}, u32[]{:S(2)}, u32[]{:S(2)}) async-start(f32[32,1,1,1,8,4,128]{6,0,5,3,2,1,4:T(8,128)} %copy.116), calls=%async_computation.7 | async-start | bytes 1048576 | tf_op jit(solution)/shard_map/all_to_all | solution.py:162
  103.7 12.9 all-to-all-start.19
  117.3 14.3 %all-to-all-start.1 = ((f32[32,1,1,1,8,4,128]{6,5,0,3,2,1,4:T(4,128)}), f32[32,1,1,1,8,4,128]{6,5,0,3,2,1,4:T(4,128)S(1)}, u32[]{:S(2)}, u32[]{:S(2)}) async-start(f32[32,1,1,1,8,4,128]{6,5,0,3,2,1,4:T(4,128)} %copy.107), calls=%async_computation.1 | async-start | bytes 1048576 | tf_op jit(solution)/shard_map/all_to_all | solution.py:155
  131.6 1.9 copy-start.3
  131.6 1.9 copy-start.13
  131.6 1.9 copy-start.14
  139.7 25.1 %all-to-all-start.22 = ((f32[32,8,1,1,1,4,128]{6,5,1,4,3,2,0:T(4,128)}), f32[32,8,1,1,1,4,128]{6,5,1,4,3,2,0:T(4,128)}, u32[]{:S(2)}, u32[]{:S(2)}) async-start(f32[32,8,1,1,1,4,128]{6,5,1,4,3,2,0:T(4,128)} %copy.142), calls=%async_computation.22 | async-start | bytes 1048576 | tf_op jit(solution)/shard_map/all_to_all | solution.py:266
  164.7 22.6 %all-to-all-start.20 = ((f32[32,8,1,1,1,4,128]{6,5,1,4,3,2,0:T(4,128)}), f32[32,8,1,1,1,4,128]{6,5,1,4,3,2,0:T(4,128)}, u32[]{:S(2)}, u32[]{:S(2)}) async-start(f32[32,8,1,1,1,4,128]{6,5,1,4,3,2,0:T(4,128)} %copy.139), calls=%async_computation.20 | async-start | bytes 1048576 | tf_op jit(solution)/shard_map/all_to_all | solution.py:257
  187.3 22.6 %all-to-all-start.10 = ((f32[32,8,1,1,1,4,128]{6,5,1,4,3,2,0:T(4,128)}), f32[32,8,1,1,1,4,128]{6,5,1,4,3,2,0:T(4,128)}, u32[]{:S(2)}, u32[]{:S(2)}) async-start(f32[32,8,1,1,1,4,128]{6,5,1,4,3,2,0:T(4,128)} %copy.121), calls=%async_computation.10 | async-start | bytes 1048576 | tf_op jit(solution)/shard_map/all_to_all | solution.py:203
  209.9 22.6 %all-to-all-start.8 = ((f32[32,8,1,1,1,4,128]{6,5,1,4,3,2,0:T(4,128)}), f32[32,8,1,1,1,4,128]{6,5,1,4,3,2,0:T(4,128)}, u32[]{:S(2)}, u32[]{:S(2)}) async-start(f32[32,8,1,1,1,4,128]{6,5,1,4,3,2,0:T(4,128)} %copy.118), calls=%async_computation.8 | async-start | bytes 1048576 | tf_op jit(solution)/shard_map/all_to_all | solution.py:194
  232.5 22.6 %all-to-all-start.4 = ((f32[32,8,1,1,1,4,128]{6,5,1,4,3,2,0:T(4,128)}), f32[32,8,1,1,1,4,128]{6,5,1,4,3,2,0:T(4,128)}, u32[]{:S(2)}, u32[]{:S(2)}) async-start(f32[32,8,1,1,1,4,128]{6,5,1,4,3,2,0:T(4,128)} %copy.112), calls=%async_computation.4 | async-start | bytes 1048576 | tf_op jit(solution)/shard_map/all_to_all | solution.py:185
  255.1 22.1 %all-to-all-start.2 = ((f32[32,8,1,1,1,4,128]{6,5,1,4,3,2,0:T(4,128)}), f32[32,8,1,1,1,4,128]{6,5,1,4,3,2,0:T(4,128)S(1)}, u32[]{:S(2)}, u32[]{:S(2)}) async-start(f32[32,8,1,1,1,4,128]{6,5,1,4,3,2,0:T(4,128)} %copy.109), calls=%async_computation.2 | async-start | bytes 1048576 | tf_op jit(solution)/shard_map/all_to_all | solution.py:176
  277.2 14.1 %all-to-all-start.23 = ((f32[1,8,1,32,1,4,128]{6,5,3,4,2,0,1:T(4,128)}), f32[1,8,1,32,1,4,128]{6,5,3,4,2,0,1:T(4,128)}, u32[]{:S(2)}, u32[]{:S(2)}) async-start(f32[1,8,1,32,1,4,128]{6,5,3,4,2,0,1:T(4,128)} %copy.143), calls=%async_computation.23 | async-start | bytes 1048576 | tf_op jit(solution)/shard_map/all_to_all | solution.py:265
  291.3 28.5 %all-to-all-start.21 = ((f32[1,8,1,32,1,4,128]{6,5,3,4,2,0,1:T(4,128)}), f32[1,8,1,32,1,4,128]{6,5,3,4,2,0,1:T(4,128)S(1)}, u32[]{:S(2)}, u32[]{:S(2)}) async-start(f32[1,8,1,32,1,4,128]{6,5,3,4,2,0,1:T(4,128)} %copy.140), calls=%async_computation.21 | async-start | bytes 1048576 | tf_op jit(solution)/shard_map/all_to_all | solution.py:256
  298.5 0.8 copy-start.15
  319.8 28.0 %all-to-all-start.11 = ((f32[1,8,1,32,1,4,128]{6,5,3,4,2,0,1:T(4,128)}), f32[1,8,1,32,1,4,128]{6,5,3,4,2,0,1:T(4,128)}, u32[]{:S(2)}, u32[]{:S(2)}) async-start(f32[1,8,1,32,1,4,128]{6,5,3,4,2,0,1:T(4,128)} %copy.122), calls=%async_computation.11 | async-start | bytes 1048576 | tf_op jit(solution)/shard_map/all_to_all | solution.py:202
  347.8 29.4 %all-to-all-start.9 = ((f32[1,8,1,32,1,4,128]{6,5,3,4,2,0,1:T(4,128)}), f32[1,8,1,32,1,4,128]{6,5,3,4,2,0,1:T(4,128)S(1)}, u32[]{:S(2)}, u32[]{:S(2)}) async-start(f32[1,8,1,32,1,4,128]{6,5,3,4,2,0,1:T(4,128)} %copy.119), calls=%async_computation.9 | async-start | bytes 1048576 | tf_op jit(solution)/shard_map/all_to_all | solution.py:193
  377.2 28.1 %all-to-all-start.5 = ((f32[1,8,1,32,1,4,128]{6,5,3,4,2,0,1:T(4,128)}), f32[1,8,1,32,1,4,128]{6,5,3,4,2,0,1:T(4,128)}, u32[]{:S(2)}, u32[]{:S(2)}) async-start(f32[1,8,1,32,1,4,128]{6,5,3,4,2,0,1:T(4,128)} %copy.113), calls=%async_computation.5 | async-start | bytes 1048576 | tf_op jit(solution)/shard_map/all_to_all | solution.py:184
  384.0 0.8 copy-start.22
  405.2 29.6 %all-to-all-start.3 = ((f32[1,8,1,32,1,4,128]{6,5,3,4,2,0,1:T(4,128)}), f32[1,8,1,32,1,4,128]{6,5,3,4,2,0,1:T(4,128)S(1)}, u32[]{:S(2)}, u32[]{:S(2)}) async-start(f32[1,8,1,32,1,4,128]{6,5,3,4,2,0,1:T(4,128)} %copy.110), calls=%async_computation.3 | async-start | bytes 1048576 | tf_op jit(solution)/shard_map/all_to_all | solution.py:175
  413.5 0.8 copy-start.24
  435.0 20.0 %copy-start.16 = (f32[1,1,1,32,8,1,4,128]{7,6,4,3,5,2,1,0:T(4,128)S(1)}, f32[1,1,1,32,8,1,4,128]{7,6,4,3,5,2,1,0:T(4,128)}, u32[]{:S(2)}) copy-start(f32[1,1,1,32,8,1,4,128]{7,6,4,3,5,2,1,0:T(4,128)} %copy-done.15) | copy-start | bytes 1572868
  435.0 20.0 %copy-start.18 = (f32[1,1,1,32,8,1,4,128]{7,6,4,3,5,2,1,0:T(4,128)S(1)}, f32[1,1,1,32,8,1,4,128]{7,6,4,3,5,2,1,0:T(4,128)}, u32[]{:S(2)}) copy-start(f32[1,1,1,32,8,1,4,128]{7,6,4,3,5,2,1,0:T(4,128)} %copy-done.17) | copy-start | bytes 1572868
  435.0 20.0 %copy-start.33 = (f32[1,1024,128]{1,2,0:T(8,128)S(1)}, f32[1,1024,128]{1,2,0:T(8,128)}, u32[]{:S(2)}) copy-start(f32[1,1024,128]{1,2,0:T(8,128)} %fusion.72) | copy-start | bytes 1572868
  435.0 20.0 %copy-start.34 = (f32[1,1024,128]{1,2,0:T(8,128)S(1)}, f32[1,1024,128]{1,2,0:T(8,128)}, u32[]{:S(2)}) copy-start(f32[1,1024,128]{1,2,0:T(8,128)} %fusion.90) | copy-start | bytes 1572868
  455.0 21.3 %copy-start.21 = (f32[1,1,1,32,8,1,4,128]{7,6,4,3,5,2,1,0:T(4,128)S(1)}, f32[1,1,1,32,8,1,4,128]{7,6,4,3,5,2,1,0:T(4,128)}, u32[]{:S(2)}) copy-start(f32[1,1,1,32,8,1,4,128]{7,6,4,3,5,2,1,0:T(4,128)} %copy-done.20) | copy-start | bytes 1572868
  455.1 21.3 %copy-start.23 = (f32[1,1,1,32,8,1,4,128]{7,6,4,3,5,2,1,0:T(4,128)S(1)}, f32[1,1,1,32,8,1,4,128]{7,6,4,3,5,2,1,0:T(4,128)}, u32[]{:S(2)}) copy-start(f32[1,1,1,32,8,1,4,128]{7,6,4,3,5,2,1,0:T(4,128)} %copy-done.22) | copy-start | bytes 1572868
  455.1 21.3 %copy-start.35 = (f32[1,1024,128]{1,2,0:T(8,128)S(1)}, f32[1,1024,128]{1,2,0:T(8,128)}, u32[]{:S(2)}) copy-start(f32[1,1024,128]{1,2,0:T(8,128)} %fusion.66) | copy-start | bytes 1572868
  455.1 21.3 %copy-start.36 = (f32[1,1024,128]{1,2,0:T(8,128)S(1)}, f32[1,1024,128]{1,2,0:T(8,128)}, u32[]{:S(2)}) copy-start(f32[1,1024,128]{1,2,0:T(8,128)} %fusion.84) | copy-start | bytes 1572868
  476.4 21.5 %copy-start.25 = (f32[1,1,1,32,8,1,4,128]{7,6,4,3,5,2,1,0:T(4,128)S(1)}, f32[1,1,1,32,8,1,4,128]{7,6,4,3,5,2,1,0:T(4,128)}, u32[]{:S(2)}) copy-start(f32[1,1,1,32,8,1,4,128]{7,6,4,3,5,2,1,0:T(4,128)} %copy-done.24) | copy-start | bytes 1572868
  476.4 21.5 %copy-start.32 = (f32[1,1024,128]{1,2,0:T(8,128)S(1)}, f32[1,1024,128]{1,2,0:T(8,128)}, u32[]{:S(2)}) copy-start(f32[1,1024,128]{1,2,0:T(8,128)} %fusion.63) | copy-start | bytes 1572868
  662.4 21.5 %copy-start.30 = (f32[1024]{0:T(1024)S(1)}, f32[1024]{0:T(1024)}, u32[]{:S(2)}) copy-start(f32[1024]{0:T(1024)} %get-tuple-element.69) | copy-start | bytes 12292
  662.4 21.5 %copy-start.31 = (f32[1024]{0:T(1024)S(1)}, f32[1024]{0:T(1024)}, u32[]{:S(2)}) copy-start(f32[1024]{0:T(1024)} %get-tuple-element.70) | copy-start | bytes 12292
  707.4 25.0 %all-to-all-start.12 = ((f32[1,1,1,32,8,4,128]{6,5,4,2,1,0,3:T(4,128)}), f32[1,1,1,32,8,4,128]{6,5,4,2,1,0,3:T(4,128)S(1)}, u32[]{:S(2)}, u32[]{:S(2)}) async-start(f32[1,1,1,32,8,4,128]{6,5,4,2,1,0,3:T(4,128)} %bitcast.346), calls=%async_computation.12 | async-start | bytes 1048576 | tf_op jit(solution)/shard_map/all_to_all | solution.py:223
  732.4 22.6 %all-to-all-start.14 = ((f32[1,1,1,32,8,4,128]{6,5,4,2,1,0,3:T(4,128)}), f32[1,1,1,32,8,4,128]{6,5,4,2,1,0,3:T(4,128)}, u32[]{:S(2)}, u32[]{:S(2)}) async-start(f32[1,1,1,32,8,4,128]{6,5,4,2,1,0,3:T(4,128)} %bitcast.345), calls=%async_computation.14 | async-start | bytes 1048576 | tf_op jit(solution)/shard_map/all_to_all | solution.py:230
  755.0 16.7 %all-to-all-start.13 = ((f32[32,1,1,1,8,4,128]{6,5,0,3,2,1,4:T(4,128)}), f32[32,1,1,1,8,4,128]{6,5,0,3,2,1,4:T(4,128)S(1)}, u32[]{:S(2)}, u32[]{:S(2)}) async-start(f32[32,1,1,1,8,4,128]{6,5,0,3,2,1,4:T(4,128)} %copy.126), calls=%async_computation.13 | async-start | bytes 1048576 | tf_op jit(solution)/shard_map/all_to_all | solution.py:222
  772.5 12.6 all-to-all-start.15
  785.1 36.1 %all-to-all-start.26 = ((f32[1,1,1,32,8,4,256]{6,0,5,4,2,1,3:T(1,128)}), f32[1,1,1,32,8,4,256]{6,0,5,4,2,1,3:T(1,128)}, u32[]{:S(2)}, u32[]{:S(2)}) async-start(f32[1,1,1,32,8,4,256]{6,0,5,4,2,1,3:T(1,128)} %bitcast.334), calls=%async_computation.26 | async-start | bytes 2097152 | tf_op jit(solution)/shard_map/all_to_all | solution.py:302
  821.2 34.0 %all-to-all-start.24 = ((f32[1,1,1,32,8,4,256]{6,0,5,4,2,1,3:T(1,128)}), f32[1,1,1,32,8,4,256]{6,0,5,4,2,1,3:T(1,128)}, u32[]{:S(2)}, u32[]{:S(2)}) async-start(f32[1,1,1,32,8,4,256]{6,0,5,4,2,1,3:T(1,128)} %bitcast.333), calls=%async_computation.24 | async-start | bytes 2097152 | tf_op jit(solution)/shard_map/all_to_all | solution.py:289
  855.2 22.1 %all-to-all-start.16 = ((f32[32,8,1,1,1,4,128]{6,5,1,4,3,2,0:T(4,128)}), f32[32,8,1,1,1,4,128]{6,5,1,4,3,2,0:T(4,128)S(1)}, u32[]{:S(2)}, u32[]{:S(2)}) async-start(f32[32,8,1,1,1,4,128]{6,5,1,4,3,2,0:T(4,128)} %copy.132), calls=%async_computation.16 | async-start | bytes 1048576 | tf_op jit(solution)/shard_map/all_to_all | solution.py:239
  877.3 20.0 %all-to-all-start.27 = ((f32[32,1,1,1,8,4,256]{6,1,5,3,2,0,4:T(1,128)}), f32[32,1,1,1,8,4,256]{6,1,5,3,2,0,4:T(1,128)}, u32[]{:S(2)}, u32[]{:S(2)}) async-start(f32[32,1,1,1,8,4,256]{6,1,5,3,2,0,4:T(1,128)} %copy.151), calls=%async_computation.27 | async-start | bytes 2097152 | tf_op jit(solution)/shard_map/all_to_all | solution.py:301
  897.3 19.1 %all-to-all-start.25 = ((f32[32,1,1,1,8,4,256]{6,1,5,3,2,0,4:T(1,128)}), f32[32,1,1,1,8,4,256]{6,1,5,3,2,0,4:T(1,128)}, u32[]{:S(2)}, u32[]{:S(2)}) async-start(f32[32,1,1,1,8,4,256]{6,1,5,3,2,0,4:T(1,128)} %copy.147), calls=%async_computation.25 | async-start | bytes 2097152 | tf_op jit(solution)/shard_map/all_to_all | solution.py:288
  916.4 12.6 all-to-all-start.17
  921.7 3.9 copy-start.2
  923.9 3.3 copy-start.12
  928.9 15.6 %copy-start.6 = (f32[1,8,1,32,1,4,128]{6,5,3,4,2,0,1:T(4,128)}, f32[1,8,1,32,1,4,128]{6,5,3,4,2,0,1:T(4,128)S(1)}, u32[]{:S(2)}) copy-start(f32[1,8,1,32,1,4,128]{6,5,3,4,2,0,1:T(4,128)S(1)} %all-to-all-done.17) | copy-start | bytes 1572868
  929.0 26.7 %all-to-all-start.30 = ((f32[32,8,1,1,1,4,128]{6,5,1,4,3,2,0:T(4,128)}), f32[32,8,1,1,1,4,128]{6,5,1,4,3,2,0:T(4,128)}, u32[]{:S(2)}, u32[]{:S(2)}) async-start(f32[32,8,1,1,1,4,128]{6,5,1,4,3,2,0:T(4,128)} %copy.156), calls=%async_computation.30 | async-start | bytes 1048576 | tf_op jit(solution)/shard_map/all_to_all | solution.py:321
  955.6 22.6 %all-to-all-start.28 = ((f32[32,8,1,1,1,4,128]{6,1,5,4,3,2,0:T(8,128)}), f32[32,8,1,1,1,4,128]{6,1,5,4,3,2,0:T(8,128)}, u32[]{:S(2)}, u32[]{:S(2)}) async-start(f32[32,8,1,1,1,4,128]{6,1,5,4,3,2,0:T(8,128)} %copy.153), calls=%async_computation.28 | async-start | bytes 1048576 | tf_op jit(solution)/shard_map/all_to_all | solution.py:330
  978.2 15.0 %all-to-all-start.31 = ((f32[1,8,1,32,1,4,128]{6,5,3,4,2,0,1:T(4,128)}), f32[1,8,1,32,1,4,128]{6,5,3,4,2,0,1:T(4,128)}, u32[]{:S(2)}, u32[]{:S(2)}) async-start(f32[1,8,1,32,1,4,128]{6,5,3,4,2,0,1:T(4,128)} %copy.157), calls=%async_computation.31 | async-start | bytes 1048576 | tf_op jit(solution)/shard_map/all_to_all | solution.py:320
  993.2 88.0 %all-to-all-start.29 = ((f32[1,8,1,32,1,4,128]{6,3,5,4,2,0,1:T(8,128)}), f32[1,8,1,32,1,4,128]{6,3,5,4,2,0,1:T(8,128)}, u32[]{:S(2)}, u32[]{:S(2)}) async-start(f32[1,8,1,32,1,4,128]{6,3,5,4,2,0,1:T(8,128)} %copy.154), calls=%async_computation.29 | async-start | bytes 1048576 | tf_op jit(solution)/shard_map/all_to_all | solution.py:329
  997.4 334.1 %all-reduce.3.cloned.1.call-start = ((), (), s32[]{:S(2)}) async-start(), calls=%async_computation.32 | async-start | bytes 524288 | tf_op jit(solution)/shard_map/psum | solution.py:356
  998.6 1.1 copy-start.4
  998.7 2.8 copy-start.10
  998.7 2.8 copy-start.5
  1001.5 77.8 %copy-start.9 = (f32[1024,128]{1,0:T(8,128)S(1)}, f32[1024,128]{1,0:T(8,128)}, u32[]{:S(2)}) copy-start(f32[1024,128]{1,0:T(8,128)} %copy-done.8) | copy-start | bytes 1572868
  1001.5 77.8 %copy-start.11 = (f32[1024,128]{1,0:T(8,128)S(1)}, f32[1024,128]{1,0:T(8,128)}, u32[]{:S(2)}) copy-start(f32[1024,128]{1,0:T(8,128)} %copy-done.10) | copy-start | bytes 1572868
  (6 other events, 4.8 us)
Sparse Core Ops, SparseCore 0:
  1083.6 247.9 all-reduce.2
where the time goes:
time: 1350 us; the launch traced here: 1340 us
  waiting for transfers between devices  527 us (39%)
  matrix products  419 us (31%)
  starting transfers between devices  189 us (14%)
  blocking collectives  99 us (7%)
  local copies, waits for them, and re-layouts  78.2 us (6%)
  between operations  15.2 us (1%)
  other arithmetic  14.3 us (1%)
    dot_general x18, matrix products, inner_apply(): jnp.einsum('kb,abc->akc', table, data, preferred_element_type=jnp.float32...  373 us
    psum x1, waiting for transfers between devices, body(): lax.psum((in_grad_local, stem_grad_local, local), ('row', 'col'))  247 us
    psum x1, blocking collectives, body(): lax.psum((in_grad_local, stem_grad_local, local), ('row', 'col'))  77.2 us
    dot_general x12, matrix products, outer_apply(): jnp.einsum('ka,abc->kbc', table, data, preferred_element_type=jnp.float32...  35.2 us
  transfers between devices with their start and end apart: 33, of which 26 were waited for; matrix products, arithmetic and copies ran while one was open for 16% of the time, Pallas kernels for 0%

commit v1 on v0

v1 whole, which is shorter than its diff:
```python
import math

import jax
import jax.numpy as jnp
from jax import lax
from jax.experimental import pallas as pl
from jax.experimental.pallas import tpu as pltpu
from jax.sharding import PartitionSpec as P

MESH = pl.DeviceIdType.MESH
F32 = jnp.float32
BF16 = jnp.bfloat16
EPSILON = 1e-05

CH = 128
LANE = 128
FR = 1024
HALF = 131072
ROWS = 528
CUT = 176
PIECE = 40
MEMBERS = 16

COS_TERMS = [(-1.0) ** i / math.factorial(2 * i) for i in range(9)]
SIN_TERMS = [(-1.0) ** i / math.factorial(2 * i + 1) for i in range(9)]


def split(x):
    high = x.astype(BF16)
    return high, (x - high.astype(F32)).astype(BF16)


def mm(a, b):
    return jnp.dot(a, b, preferred_element_type=F32)


def mm_nt(a, b):
    return lax.dot_general(a, b, (((1,), (1,)), ((), ())), preferred_element_type=F32)


def dot3(a, b, form=mm):
    (ah, al), (bh, bl) = a, b
    return form(ah, bh) + (form(al, bh) + form(ah, bl))


def sincos(index, period):
    half = period // 2
    x = (((index + half) & (period - 1)) - half).astype(F32) * (2.0 * math.pi / period)
    x2 = x * x
    c = jnp.full_like(x, COS_TERMS[-1])
    s = jnp.full_like(x, SIN_TERMS[-1])
    for term in COS_TERMS[-2::-1]:
        c = c * x2 + term
    for term in SIN_TERMS[-2::-1]:
        s = s * x2 + term
    return c, s * x


def iota(shape, dim):
    return lax.broadcasted_iota(jnp.int32, shape, dim)


def aligned(start, size, unit=8):
    return pl.ds(pl.multiple_of(start, unit), size)


def kernel(
    samples, stem_w, in_w, filt, out_w, cot,
    layer_out, filter_grad, stem_grad, in_grad, out_grad,
    s0, s1, s2, r0, r1, r2, x0, x1, x2, x3, x4, x5, c0, c1, c2, h0, h1, h2, o0, o1, o2,
    f1h, f1l, gh, gl, w2h, w2l, v2h, v2l, twc, tws,
    rhs2, yr, yi, spec,
    edge, win, stem, normed, qkv, gg,
    swh, swl, iwh, iwl, owh, owl,
    gsum, rs_in, red, ag_in, tot, fin,
    send_sem, recv_sem, xsend, xrecv, esend, erecv, rsend, rrecv,
):
    sbuf, rbuf, xbuf = (s0, s1, s2), (r0, r1, r2), (x0, x1, x2, x3, x4, x5)
    cbuf, hbuf, obuf = (c0, c1, c2), (h0, h1, h2), (o0, o1, o2)
    row, col = lax.axis_index("row"), lax.axis_index("col")
    core = row % 2
    half = row // 16
    chip = (row // 2) * 8 + col
    place = (row % 16) * 8 + col
    dev = row * 8 + col
    partner = (row + 1 - 2 * core, col)
    sign = (1 - 2 * core).astype(F32)
    own_half = half == core

    def tile(k):
        return aligned(k * 8, 8)

    def scatter(src, dst, unit, slot, own, target):
        def one(i, carry):
            k = (own + 1 + i) % CH
            pltpu.make_async_remote_copy(
                src.at[tile(k)], dst.at[tile(slot)], send_sem.at[unit], recv_sem.at[unit],
                device_id=target(k), device_id_type=MESH,
            ).start()
            return carry

        lax.fori_loop(0, CH - 1, one, 0)

        @pl.when(own_half)
        def _():
            pltpu.make_async_copy(src.at[tile(own)], dst.at[tile(slot)], recv_sem.at[unit]).start()

        @pl.when(jnp.logical_not(own_half))
        def _():
            pltpu.make_async_remote_copy(
                src.at[tile(own)], dst.at[tile(slot)], send_sem.at[unit], recv_sem.at[unit],
                device_id=target(own), device_id_type=MESH,
            ).start()

    def arrived(dst, unit):
        pltpu.make_async_copy(dst, dst, recv_sem.at[unit]).wait()

    def sent(src, unit):
        @pl.when(own_half)
        def _():
            part = src.at[pl.ds(0, FR - 8)]
            pltpu.make_async_copy(part, part, send_sem.at[unit]).wait()

        @pl.when(jnp.logical_not(own_half))
        def _():
            pltpu.make_async_copy(src, src, send_sem.at[unit]).wait()

    def to_chip(k):
        return ((k // 8) * 2 + half, k % 8)

    def to_frames(k):
        return (k // 8 + 16 * core, k % 8)

    def scatter_in(unit):
        scatter(sbuf[unit], rbuf[unit], unit, place, chip, to_chip)

    def scatter_out(unit):
        scatter(hbuf[unit], obuf[unit], 3 + unit, chip, place, to_frames)

    @pl.when(dev > 0)
    def _():
        pltpu.make_async_remote_copy(
            samples.at[pl.ds(0, 8)], edge, esend, erecv,
            device_id=((dev - 1) // 8, (dev + 7) % 8), device_id_type=MESH,
        ).start()

    def put_rows(unit, r, block):
        sbuf[unit][pl.ds(r, CH, stride=8), :] = block.T

    def filter_block(r, carry):
        put_rows(0, r, filt[aligned(r * LANE, LANE, LANE), :])
        return carry

    lax.fori_loop(0, 8, filter_block, 0)
    scatter_in(0)

    for src, high, low in ((stem_w, swh, swl), (in_w, iwh, iwl), (out_w, owh, owl)):
        h, l = split(src[...])
        high[...] = h
        low[...] = l

    @pl.when(dev == 255)
    def _():
        edge[...] = jnp.zeros_like(edge)

    @pl.when(dev < 255)
    def _():
        pltpu.make_async_copy(edge, edge, erecv).wait()

    own = samples[...]
    following = jnp.where(
        iota((LANE, LANE), 0) == LANE - 1, edge[0:1, :], pltpu.roll(own, LANE - 1, 0)
    )
    for q in range(8):
        if q == 0:
            window = own
        elif q < 7:
            window = pltpu.roll(own, LANE - 16 * q, 1)
        else:
            window = jnp.where(
                iota((LANE, LANE), 1) < 16, pltpu.roll(own, 16, 1), pltpu.roll(following, 16, 1)
            )
        win[pl.ds(q, LANE, stride=8), :] = window

    def forward_block(r, carry):
        here = aligned(r * LANE, LANE, LANE)
        stem_out = dot3(split(win[here, :]), (swh[...], swl[...]))
        scale = lax.rsqrt(jnp.mean(stem_out * stem_out, axis=1, keepdims=True) + EPSILON)
        norm = stem_out * scale
        proj = dot3(split(norm), (iwh[...], iwl[...]))
        stem[here, :] = stem_out
        normed[here, :] = norm
        qkv[here, :] = proj
        put_rows(1, r, proj[:, CH : 2 * CH] * proj[:, 2 * CH :])
        return carry

    lax.fori_loop(0, 8, forward_block, 0)
    scatter_in(1)

    def grad_block(r, carry):
        here = aligned(r * LANE, LANE, LANE)
        gated_grad = dot3(split(cot[here, :]), (owh[...], owl[...]), mm_nt)
        gg[here, :] = gated_grad
        put_rows(2, r, gated_grad * qkv[here, 0:CH])
        return carry

    lax.fori_loop(0, 8, grad_block, 0)
    scatter_in(2)

    def f1_block(b, carry):
        k1 = iota((16, FR), 0) + b * 16
        c, s = sincos(iota((16, FR), 1) * (2 * k1 + core), 2048)
        h, l = split(c)
        f1h[aligned(b * 16, 16, 16), :] = h
        f1l[aligned(b * 16, 16, 16), :] = l
        h, l = split(-s)
        f1h[aligned(512 + b * 16, 16, 16), :] = h
        f1l[aligned(512 + b * 16, 16, 16), :] = l
        return carry

    lax.fori_loop(0, 32, f1_block, 0)

    def tw_block(b, carry):
        here = aligned(b * 16, 16, 16)
        k1 = iota((16, LANE), 0) + b * 16
        c, s = sincos(iota((16, LANE), 1) * (2 * k1 + core), 2 * HALF)
        twc[here, :] = c
        tws[here, :] = -s
        return carry

    lax.fori_loop(0, ROWS // 16, tw_block, 0)

    cc, ss = sincos(iota((LANE, LANE), 0) * iota((LANE, LANE), 1), LANE)
    for (i, j), fwd, inv in (((0, 0), cc, cc), ((0, 1), -ss, ss), ((1, 0), ss, -ss), ((1, 1), cc, cc)):
        box = (slice(i * LANE, (i + 1) * LANE), slice(j * LANE, (j + 1) * LANE))
        w2h[box], w2l[box] = split(fwd)
        v2h[box], v2l[box] = split(inv)

    def g_block(b, carry):
        here = aligned(b * 16, 16, 16)
        n1 = iota((16, 512), 0) + b * 16
        c, s = sincos(n1 * (2 * iota((16, 512), 1) + core), 2048)
        gh[here, 0:512], gl[here, 0:512] = split(c)
        gh[here, 512:], gl[here, 512:] = split(-s)
        return carry

    lax.fori_loop(0, FR // 16, g_block, 0)

    odd = (1 - 2 * (iota((FR, LANE), 0) % 2)).astype(F32)

    def exchange(src, slot):
        pltpu.make_async_remote_copy(
            src, xbuf[slot], xsend.at[slot], xrecv.at[slot],
            device_id=partner, device_id_type=MESH,
        ).start()

    def exchanged(slot):
        pltpu.make_async_copy(xbuf[slot], xbuf[slot], xrecv.at[slot]).wait()

    def table_product(high, low, b):
        here = aligned(b * 512, 512, 512)
        both = mm(high[here, :], rhs2[...])
        return both[:, :LANE] + (both[:, LANE:] + mm(low[here, :], rhs2[:, :LANE]))

    def transform(unit):
        arrived(rbuf[unit], unit)
        exchange(rbuf[unit], unit)
        exchanged(unit)
        data = xbuf[unit][...] + sign * rbuf[unit][...]
        h, l = split(data)
        rhs2[:, :LANE] = h
        rhs2[:, LANE:] = l
        middle = jnp.sum(data * odd, axis=0, keepdims=True)
        yr[512:, :] = jnp.where(iota((16, LANE), 0) == 0, middle, 0.0)
        yi[512:, :] = jnp.zeros((16, LANE), F32)
        yr[0:512, :] = table_product(f1h, f1l, 0)
        yi[0:512, :] = table_product(f1h, f1l, 1)

        def second(b, carry):
            here = aligned(b * CUT, CUT, 16)
            a, bb, c, s = yr[here, :], yi[here, :], twc[here, :], tws[here, :]
            turned = jnp.concatenate([a * c - bb * s, a * s + bb * c], axis=1)
            spec[unit, here, :] = dot3(split(turned), (w2h[...], w2l[...]))
            return carry

        lax.fori_loop(0, ROWS // CUT, second, 0)

    def inverse(unit, product):
        def second(b, carry):
            here = aligned(b * CUT, CUT, 16)
            z = dot3(split(product(here)), (v2h[...], v2l[...]))
            zr, zi = z[:, :LANE], z[:, LANE:]
            c, s = twc[here, :], tws[here, :]
            k1 = iota((CUT, LANE), 0) + b * CUT
            single = (k1 == 0) | (k1 == 512)
            weight = jnp.where(core == 0, jnp.where(single, 1.0, 2.0), jnp.where(k1 < 512, 2.0, 0.0))
            weight = weight * (2.0 ** -27)
            yr[here, :] = (zr * c + zi * s) * weight
            yi[here, :] = (zi * c - zr * s) * weight
            return carry

        lax.fori_loop(0, ROWS // CUT, second, 0)
        for part, base in ((yr, 0), (yi, 512)):
            h, l = split(part[0:512, :])
            rhs2[base : base + 512, :LANE] = h
            rhs2[base : base + 512, LANE:] = l
        middle = yr[512:513, :]
        for b in range(2):
            here = slice(b * 512, (b + 1) * 512)
            cbuf[unit][here, :] = table_product(gh, gl, b) + odd[here, :] * middle
        exchange(cbuf[unit], 3 + unit)
        exchanged(3 + unit)
        hbuf[unit][...] = xbuf[3 + unit][...] + sign * cbuf[unit][...]
        scatter_out(unit)

    def times(a, b, here):
        x, y = spec[a, here, :], spec[b, here, :]
        ar, ai, br, bi = x[:, :LANE], x[:, LANE:], y[:, :LANE], y[:, LANE:]
        return ar, ai, br, bi

    def plain(a, b):
        def product(here):
            ar, ai, br, bi = times(a, b, here)
            return jnp.concatenate([ar * br - ai * bi, ar * bi + ai * br], axis=1)

        return product

    def conjugate(a, b):
        def product(here):
            ar, ai, br, bi = times(a, b, here)
            return jnp.concatenate([ar * br + ai * bi, ar * bi - ai * br], axis=1)

        return product

    transform(0)
    transform(1)
    inverse(0, plain(0, 1))
    transform(2)
    inverse(1, conjugate(0, 2))
    inverse(2, conjugate(1, 2))

    gsum[...] = jnp.zeros_like(gsum)

    def frames_of(unit, r):
        return obuf[unit][pl.ds(r, CH, stride=8), :].T

    arrived(obuf[0], 3)

    def conv_block(r, carry):
        here = aligned(r * LANE, LANE, LANE)
        conv = frames_of(0, r)
        gated = qkv[here, 0:CH] * conv
        layer_out[here, :] = dot3(split(gated), (owh[...], owl[...])) + stem[here, :]
        gsum[384:512, :] += dot3(split(gated.T), split(cot[here, :]))
        gg[here, :] = gg[here, :] * conv
        return carry

    lax.fori_loop(0, 8, conv_block, 0)

    arrived(obuf[1], 4)

    def back_block(r, carry):
        here = aligned(r * LANE, LANE, LANE)
        input_grad = frames_of(1, r)
        norm = normed[here, :]
        proj_grad = split(
            jnp.concatenate(
                [gg[here, :], input_grad * qkv[here, 2 * CH :], input_grad * qkv[here, CH : 2 * CH]],
                axis=1,
            )
        )
        grads = dot3(split(norm.T), proj_grad)
        for i in range(3):
            gsum[i * CH : (i + 1) * CH, :] += grads[:, i * CH : (i + 1) * CH]
        normed_grad = dot3(proj_grad, (iwh[...], iwl[...]), mm_nt)
        stem_out = stem[here, :]
        scale = lax.rsqrt(jnp.mean(stem_out * stem_out, axis=1, keepdims=True) + EPSILON)
        along = jnp.mean(norm * normed_grad, axis=1, keepdims=True)
        stem_out_grad = cot[here, :] + scale * (normed_grad - norm * along)
        gsum[512:544, :] += dot3(split(win[here, :].T), split(stem_out_grad))[0:32, :]
        return carry

    lax.fori_loop(0, 8, back_block, 0)

    z, x_lo = row // 4, (row // 2) % 2
    first, second_place = z * 2 + core, x_lo * 8 + col

    def share(step, src, dst, own_place, target):
        def one(i, carry):
            m = (own_place + 1 + i) % MEMBERS
            pltpu.make_async_remote_copy(
                src(m), dst.at[own_place], rsend.at[step], rrecv.at[step],
                device_id=target(m), device_id_type=MESH,
            ).start()
            return carry

        lax.fori_loop(0, MEMBERS - 1, one, 0)
        pltpu.make_async_copy(src(own_place), dst.at[own_place], rrecv.at[step]).start()
        pltpu.make_async_copy(dst, dst, rrecv.at[step]).wait()

    def in_first(m):
        return ((m // 2) * 4 + x_lo * 2 + m % 2, col)

    def in_second(m):
        return (z * 4 + (m // 8) * 2 + core, m % 8)

    share(0, lambda m: gsum.at[aligned(m * PIECE, PIECE)], rs_in, first, in_first)
    red[...] = jnp.sum(rs_in[...], axis=0)
    share(1, lambda m: red, ag_in, second_place, in_second)
    tot[...] = jnp.sum(ag_in[...], axis=0) * (2.0 ** -9)
    share(2, lambda m: tot, fin, first, in_first)

    def summed(start, size, out, columns):
        done = 0
        while done < size:
            piece, offset = divmod(start + done, PIECE)
            count = min(PIECE - offset, size - done)
            out[done : done + count, columns] = fin[piece, offset : offset + count, :]
            done += count

    for i in range(3):
        summed(i * CH, CH, in_grad, slice(i * CH, (i + 1) * CH))
    summed(384, CH, out_grad, slice(0, CH))
    summed(512, 32, stem_grad, slice(0, CH))

    arrived(obuf[2], 5)

    def filter_grad_block(r, carry):
        filter_grad[aligned(r * LANE, LANE, LANE), :] = frames_of(2, r)
        return carry

    lax.fori_loop(0, 8, filter_grad_block, 0)

    for unit in range(3):
        sent(sbuf[unit], unit)
        sent(hbuf[unit], 3 + unit)
        pltpu.make_async_copy(rbuf[unit], rbuf[unit], xsend.at[unit]).wait()
        pltpu.make_async_copy(cbuf[unit], cbuf[unit], xsend.at[3 + unit]).wait()
    for step in range(3):
        part = fin.at[pl.ds(0, MEMBERS - 1)]
        pltpu.make_async_copy(part, part, rsend.at[step]).wait()

    @pl.when(dev > 0)
    def _():
        pltpu.make_async_copy(edge, edge, esend).wait()


def body(samples, stem_weight, in_weight, filter_param, out_weight, cotangent):
    vmem = pl.BlockSpec(memory_space=pltpu.VMEM)
    stem_padded = jnp.pad(stem_weight, ((0, CH - stem_weight.shape[0]), (0, 0)))
    return pl.pallas_call(
        kernel,
        out_shape=(
            jax.ShapeDtypeStruct((FR, CH), F32),
            jax.ShapeDtypeStruct((FR, CH), F32),
            jax.ShapeDtypeStruct((32, CH), F32),
            jax.ShapeDtypeStruct((CH, 3 * CH), F32),
            jax.ShapeDtypeStruct((CH, CH), F32),
        ),
        in_specs=[vmem] * 6,
        out_specs=(vmem,) * 5,
        scratch_shapes=[
            *[pltpu.VMEM((FR, LANE), F32)] * 21,
            pltpu.VMEM((FR, FR), BF16), pltpu.VMEM((FR, FR), BF16),
            pltpu.VMEM((FR, FR), BF16), pltpu.VMEM((FR, FR), BF16),
            pltpu.VMEM((256, 256), BF16), pltpu.VMEM((256, 256), BF16),
            pltpu.VMEM((256, 256), BF16), pltpu.VMEM((256, 256), BF16),
            pltpu.VMEM((ROWS, LANE), F32), pltpu.VMEM((ROWS, LANE), F32),
            pltpu.VMEM((FR, 256), BF16),
            pltpu.VMEM((ROWS, LANE), F32), pltpu.VMEM((ROWS, LANE), F32),
            pltpu.VMEM((3, ROWS, 256), F32),
            pltpu.VMEM((8, LANE), F32),
            pltpu.VMEM((FR, LANE), F32), pltpu.VMEM((FR, LANE), F32), pltpu.VMEM((FR, LANE), F32),
            pltpu.VMEM((FR, 3 * CH), F32), pltpu.VMEM((FR, LANE), F32),
            pltpu.VMEM((CH, CH), BF16), pltpu.VMEM((CH, CH), BF16),
            pltpu.VMEM((CH, 3 * CH), BF16), pltpu.VMEM((CH, 3 * CH), BF16),
            pltpu.VMEM((CH, CH), BF16), pltpu.VMEM((CH, CH), BF16),
            pltpu.VMEM((MEMBERS * PIECE, LANE), F32), pltpu.VMEM((MEMBERS, PIECE, LANE), F32),
            pltpu.VMEM((PIECE, LANE), F32), pltpu.VMEM((MEMBERS, PIECE, LANE), F32),
            pltpu.VMEM((PIECE, LANE), F32), pltpu.VMEM((MEMBERS, PIECE, LANE), F32),
            pltpu.SemaphoreType.DMA((6,)), pltpu.SemaphoreType.DMA((6,)),
            pltpu.SemaphoreType.DMA((6,)), pltpu.SemaphoreType.DMA((6,)),
            pltpu.SemaphoreType.DMA, pltpu.SemaphoreType.DMA,
            pltpu.SemaphoreType.DMA((3,)), pltpu.SemaphoreType.DMA((3,)),
        ],
        compiler_params=pltpu.CompilerParams(has_side_effects=True, vmem_limit_bytes=60 * 2**20),
    )(samples.reshape(LANE, LANE), stem_padded, in_weight, filter_param, out_weight, cotangent)


def solution(mesh):
    in_specs = (P(("row", "col")), P(), P(), P(("row", "col"), None), P(), P(("row", "col"), None))
    out_specs = (P(("row", "col"), None), P(("row", "col"), None), P(), P(), P())
    return jax.shard_map(body, mesh=mesh, in_specs=in_specs, out_specs=out_specs, check_vma=False)
```

time: 1350 us -> 129 us (0.10)
  waiting for transfers between devices: 527 us -> 0 us
  matrix products: 419 us -> 0 us
  starting transfers between devices: 189 us -> 0 us
  Pallas kernels: 0 us -> 122 us
  blocking collectives: 99 us -> 0 us
  local copies, waits for them, and re-layouts: 78.2 us -> 6.18 us
  between operations: 15.2 us -> 0.65 us
  other arithmetic: 14.3 us -> 0 us
    dot_general x38 -> x0, matrix products: 419 us -> none  [the longest x18 373 us: inner_apply(): jnp.einsum('kb,abc->akc', table, data, preferred_element_type=jnp.float32...]
    all_to_all x31 -> x0, waiting for transfers between devices: 279 us -> none  [the longest x1 22.1 us: body(): lax.all_to_all(spread_form(jnp.concatenate([input_turned[1], weight_turne...]
    psum x1 -> x0, waiting for transfers between devices: 247 us -> none  [body(): lax.psum((in_grad_local, stem_grad_local, local), ('row', 'col'))]
    all_to_all x31 -> x0, starting transfers between devices: 180 us -> none  [the longest x1 10.2 us: body(): lax.all_to_all(collect_form(first_cols), 'row', split_axis=0, concat_axis...]
    pallas_call x0 -> x1, Pallas kernels: none -> 122 us  [body(): pl.pallas_call(kernel, out_shape=(jax.ShapeDtypeStruct((FR, CH), F32), ja...]
    psum x1 -> x0, blocking collectives: 77.2 us -> none  [body(): lax.psum((in_grad_local, stem_grad_local, local), ('row', 'col'))]
    all_to_all x26 -> x0, local copies, waits for them, and re-layouts: 39.7 us -> none  [the longest x1 3 us: body(): lax.all_to_all(spread_form(jnp.concatenate([input_turned[0], weight_turne...]
    all_to_all x1 -> x0, blocking collectives: 21.9 us -> none  [body(): lax.all_to_all(spread_form(conv_grad), 'row', split_axis=3, concat_axis=0...]
  transfers between devices with their start and end apart: 33 -> 0, of which waited for: 26 -> 0; matrix products, arithmetic and copies ran while one was open for 16% -> 0% of each run, Pallas kernels for 0% -> 0%
where the time goes in v1:
time: 129 us
  Pallas kernels  122 us (95%)
  local copies, waits for them, and re-layouts  6.18 us (5%)
    pallas_call x1, Pallas kernels, body(): pl.pallas_call(kernel, out_shape=(jax.ShapeDtypeStruct((FR, CH), F32), ja...  122 us
    unnamed x13, local copies, waits for them, and re-layouts  4.83 us

profile of v1, /device:TPU:1, one launch (start us, length us, event | category | flops | bytes accessed | tf_op | source)
XLA Modules:
  0.0 129.1 jit_solution(4272367662659419745)
XLA Ops:
  0.6 1.4 %pad.4.stem_w = f32[128,128]{1,0:T(8,128)} pad(f32[32,128]{1,0:T(8,128)} %param.7, f32[]{:T(128)} %constant.2.clone.1), padding=0_96x0_0 | pad | bytes 81924 | tf_op jit(solution)/shard_map/jit(_pad)/pad | solution.py:450
  2.0 122.2 %shard_map.101 = (f32[1024,128]{1,0:T(8,128)}, f32[1024,128]{1,0:T(8,128)}, f32[32,128]{1,0:T(8,128)}, f32[128,384]{1,0:T(8,128)}, f32[128,128]{1,0:T(8,128)}) custom-call(f32[128,128]{1,0:T(8,128)} %bitcast.1, f32[128,128]{1,0:T(8,128)} %pad.4.stem_w, f32[128,384]{1,0:T(8,128)} %in_w.1, f32[1024,128]{1,0:T(8,128)} %filt.1, f32[128,128]{1,0:T(8,128)} %out_w.1, ...), custom_call_target="tpu_custom_call" | custom-call | tf_op jit(solution)/shard_map/pallas_call | solution.py:451
  124.2 0.0 copy-start
  124.2 1.9 %copy.16 = f32[1024,128]{1,0:T(8,128)} copy(f32[1024,128]{1,0:T(8,128)} %get-tuple-element.10) | data formatting | bytes 1048576
  126.2 0.0 copy-done
  126.2 0.0 copy-start.3
  126.2 0.0 copy-start.1
  126.2 0.8 copy.17
  127.0 0.0 copy-done.3
  127.0 0.6 copy.18
  127.6 0.0 copy-done.1
  127.6 0.0 copy-start.2
  127.6 0.7 copy.19
  128.3 0.2 copy-done.2
  128.5 0.6 copy.20
Async XLA Ops:
  124.2 1.9 %copy-start = (f32[1024,128]{1,0:T(8,128)S(1)}, f32[1024,128]{1,0:T(8,128)}, u32[]{:S(2)}) copy-start(f32[1024,128]{1,0:T(8,128)} %get-tuple-element.11) | copy-start | bytes 1572868
  126.2 0.8 copy-start.3
  126.2 1.4 %copy-start.1 = (f32[128,384]{1,0:T(8,128)S(1)}, f32[128,384]{1,0:T(8,128)}, u32[]{:S(2)}) copy-start(f32[128,384]{1,0:T(8,128)} %get-tuple-element.13) | copy-start | bytes 589828
  127.6 0.9 copy-start.2

commit v2 on v1

--- a/solution.py
+++ b/solution.py
@@ -66,14 +66,14 @@
 
 def kernel(
     samples, stem_w, in_w, filt, out_w, cot,
-    layer_out, filter_grad, stem_grad, in_grad, out_grad,
+    rows_out, columns_out, sums,
     s0, s1, s2, r0, r1, r2, x0, x1, x2, x3, x4, x5, c0, c1, c2, h0, h1, h2, o0, o1, o2,
     f1h, f1l, gh, gl, w2h, w2l, v2h, v2l, twc, tws,
     rhs2, yr, yi, spec,
     edge, win, stem, normed, qkv, gg,
     swh, swl, iwh, iwl, owh, owl,
     gsum, rs_in, red, ag_in, tot, fin,
-    send_sem, recv_sem, xsend, xrecv, esend, erecv, rsend, rrecv,
+    send_sem, recv_sem, xsend, xrecv, esend, erecv, rsend, rrecv, known,
 ):
     sbuf, rbuf, xbuf = (s0, s1, s2), (r0, r1, r2), (x0, x1, x2, x3, x4, x5)
     cbuf, hbuf, obuf = (c0, c1, c2), (h0, h1, h2), (o0, o1, o2)
@@ -137,6 +137,99 @@
     def scatter_out(unit):
         scatter(hbuf[unit], obuf[unit], 3 + unit, chip, place, to_frames)
 
+    z, x_lo = row // 4, (row // 2) % 2
+    first, second_place = z * 2 + core, x_lo * 8 + col
+
+    def in_first(m):
+        return ((m // 2) * 4 + x_lo * 2 + m % 2, col)
+
+    def in_second(m):
+        return (z * 4 + (m // 8) * 2 + core, m % 8)
+
+    def make_tables():
+        def f1_block(b, carry):
+            k1 = iota((16, FR), 0) + b * 16
+            c, s = sincos(iota((16, FR), 1) * (2 * k1 + core), 2048)
+            h, l = split(c)
+            f1h[aligned(b * 16, 16, 16), :] = h
+            f1l[aligned(b * 16, 16, 16), :] = l
+            h, l = split(-s)
+            f1h[aligned(512 + b * 16, 16, 16), :] = h
+            f1l[aligned(512 + b * 16, 16, 16), :] = l
+            return carry
+
+        lax.fori_loop(0, 32, f1_block, 0)
+
+        def tw_block(b, carry):
+            here = aligned(b * 16, 16, 16)
+            k1 = iota((16, LANE), 0) + b * 16
+            c, s = sincos(iota((16, LANE), 1) * (2 * k1 + core), 2 * HALF)
+            twc[here, :] = c
+            tws[here, :] = -s
+            return carry
+
+        lax.fori_loop(0, ROWS // 16, tw_block, 0)
+
+        cc, ss = sincos(iota((LANE, LANE), 0) * iota((LANE, LANE), 1), LANE)
+        for (i, j), fwd, inv in (((0, 0), cc, cc), ((0, 1), -ss, ss), ((1, 0), ss, -ss), ((1, 1), cc, cc)):
+            box = (slice(i * LANE, (i + 1) * LANE), slice(j * LANE, (j + 1) * LANE))
+            w2h[box], w2l[box] = split(fwd)
+            v2h[box], v2l[box] = split(inv)
+
+        def g_block(b, carry):
+            here = aligned(b * 16, 16, 16)
+            n1 = iota((16, 512), 0) + b * 16
+            c, s = sincos(n1 * (2 * iota((16, 512), 1) + core), 2048)
+            gh[here, 0:512], gl[here, 0:512] = split(c)
+            gh[here, 512:], gl[here, 512:] = split(-s)
+            return carry
+
+        lax.fori_loop(0, FR // 16, g_block, 0)
+
+    barrier = pltpu.get_barrier_semaphore()
+
+    def greet(i, carry):
+        pl.semaphore_signal(
+            barrier, 1, device_id=in_first((first + 1 + i) % MEMBERS), device_id_type=MESH
+        )
+        pl.semaphore_signal(
+            barrier, 1, device_id=in_second((second_place + 1 + i) % MEMBERS), device_id_type=MESH
+        )
+        return carry
+
+    lax.fori_loop(0, MEMBERS - 1, greet, 0)
+
+    def put_rows(unit, r, block):
+        sbuf[unit][pl.ds(r, CH, stride=8), :] = block.T
+
+    def filter_block(r, carry):
+        put_rows(0, r, filt[aligned(r * LANE, LANE, LANE), :])
+        return carry
+
+    lax.fori_loop(0, 8, filter_block, 0)
+
+    for part in (swh, swl):
+        part[...] = jnp.zeros_like(part)
+    h, l = split(stem_w[...])
+    swh[0:32, :] = h
+    swl[0:32, :] = l
+    for src, high, low in ((in_w, iwh, iwl), (out_w, owh, owl)):
+        h, l = split(src[...])
+        high[...] = h
+        low[...] = l
+
+    pl.semaphore_wait(barrier, 2 * (MEMBERS - 1))
+
+    def confirm(i, carry):
+        pl.semaphore_signal(
+            known, 1, device_id=in_second((second_place + 1 + i) % MEMBERS), device_id_type=MESH
+        )
+        return carry
+
+    lax.fori_loop(0, MEMBERS - 1, confirm, 0)
+    make_tables()
+    pl.semaphore_wait(known, MEMBERS - 1)
+
     @pl.when(dev > 0)
     def _():
         pltpu.make_async_remote_copy(
@@ -144,20 +237,7 @@
             device_id=((dev - 1) // 8, (dev + 7) % 8), device_id_type=MESH,
         ).start()
 
-    def put_rows(unit, r, block):
-        sbuf[unit][pl.ds(r, CH, stride=8), :] = block.T
-
-    def filter_block(r, carry):
-        put_rows(0, r, filt[aligned(r * LANE, LANE, LANE), :])
-        return carry
-
-    lax.fori_loop(0, 8, filter_block, 0)
     scatter_in(0)
-
-    for src, high, low in ((stem_w, swh, swl), (in_w, iwh, iwl), (out_w, owh, owl)):
-        h, l = split(src[...])
-        high[...] = h
-        low[...] = l
 
     @pl.when(dev == 255)
     def _():
@@ -207,45 +287,6 @@
     lax.fori_loop(0, 8, grad_block, 0)
     scatter_in(2)
 
-    def f1_block(b, carry):
-        k1 = iota((16, FR), 0) + b * 16
-        c, s = sincos(iota((16, FR), 1) * (2 * k1 + core), 2048)
-        h, l = split(c)
-        f1h[aligned(b * 16, 16, 16), :] = h
-        f1l[aligned(b * 16, 16, 16), :] = l
-        h, l = split(-s)
-        f1h[aligned(512 + b * 16, 16, 16), :] = h
-        f1l[aligned(512 + b * 16, 16, 16), :] = l
-        return carry
-
-    lax.fori_loop(0, 32, f1_block, 0)
-
-    def tw_block(b, carry):
-        here = aligned(b * 16, 16, 16)
-        k1 = iota((16, LANE), 0) + b * 16
-        c, s = sincos(iota((16, LANE), 1) * (2 * k1 + core), 2 * HALF)
-        twc[here, :] = c
-        tws[here, :] = -s
-        return carry
-
-    lax.fori_loop(0, ROWS // 16, tw_block, 0)
-
-    cc, ss = sincos(iota((LANE, LANE), 0) * iota((LANE, LANE), 1), LANE)
-    for (i, j), fwd, inv in (((0, 0), cc, cc), ((0, 1), -ss, ss), ((1, 0), ss, -ss), ((1, 1), cc, cc)):
-        box = (slice(i * LANE, (i + 1) * LANE), slice(j * LANE, (j + 1) * LANE))
-        w2h[box], w2l[box] = split(fwd)
-        v2h[box], v2l[box] = split(inv)
-
-    def g_block(b, carry):
-        here = aligned(b * 16, 16, 16)
-        n1 = iota((16, 512), 0) + b * 16
-        c, s = sincos(n1 * (2 * iota((16, 512), 1) + core), 2048)
-        gh[here, 0:512], gl[here, 0:512] = split(c)
-        gh[here, 512:], gl[here, 512:] = split(-s)
-        return carry
-
-    lax.fori_loop(0, FR // 16, g_block, 0)
-
     odd = (1 - 2 * (iota((FR, LANE), 0) % 2)).astype(F32)
 
     def exchange(src, slot):
@@ -350,7 +391,7 @@
         here = aligned(r * LANE, LANE, LANE)
         conv = frames_of(0, r)
         gated = qkv[here, 0:CH] * conv
-        layer_out[here, :] = dot3(split(gated), (owh[...], owl[...])) + stem[here, :]
+        rows_out[here, :] = dot3(split(gated), (owh[...], owl[...])) + stem[here, :]
         gsum[384:512, :] += dot3(split(gated.T), split(cot[here, :]))
         gg[here, :] = gg[here, :] * conv
         return carry
@@ -382,9 +423,6 @@
 
     lax.fori_loop(0, 8, back_block, 0)
 
-    z, x_lo = row // 4, (row // 2) % 2
-    first, second_place = z * 2 + core, x_lo * 8 + col
-
     def share(step, src, dst, own_place, target):
         def one(i, carry):
             m = (own_place + 1 + i) % MEMBERS
@@ -398,38 +436,18 @@
         pltpu.make_async_copy(src(own_place), dst.at[own_place], rrecv.at[step]).start()
         pltpu.make_async_copy(dst, dst, rrecv.at[step]).wait()
 
-    def in_first(m):
-        return ((m // 2) * 4 + x_lo * 2 + m % 2, col)
-
-    def in_second(m):
-        return (z * 4 + (m // 8) * 2 + core, m % 8)
-
     share(0, lambda m: gsum.at[aligned(m * PIECE, PIECE)], rs_in, first, in_first)
     red[...] = jnp.sum(rs_in[...], axis=0)
     share(1, lambda m: red, ag_in, second_place, in_second)
     tot[...] = jnp.sum(ag_in[...], axis=0) * (2.0 ** -9)
     share(2, lambda m: tot, fin, first, in_first)
 
-    def summed(start, size, out, columns):
-        done = 0
-        while done < size:
-            piece, offset = divmod(start + done, PIECE)
-            count = min(PIECE - offset, size - done)
-            out[done : done + count, columns] = fin[piece, offset : offset + count, :]
-            done += count
-
-    for i in range(3):
-        summed(i * CH, CH, in_grad, slice(i * CH, (i + 1) * CH))
-    summed(384, CH, out_grad, slice(0, CH))
-    summed(512, 32, stem_grad, slice(0, CH))
+    for m in range(MEMBERS):
+        sums[m * PIECE : (m + 1) * PIECE, :] = fin[m]
 
     arrived(obuf[2], 5)
 
-    def filter_grad_block(r, carry):
-        filter_grad[aligned(r * LANE, LANE, LANE), :] = frames_of(2, r)
-        return carry
-
-    lax.fori_loop(0, 8, filter_grad_block, 0)
+    columns_out[...] = obuf[2][...]
 
     for unit in range(3):
         sent(sbuf[unit], unit)
@@ -445,20 +463,31 @@
         pltpu.make_async_copy(edge, edge, esend).wait()
 
 
+def finish(rows_in, columns_in, sums, layer_out, filter_grad, stem_grad, in_grad, out_grad):
+    layer_out[...] = rows_in[...]
+
+    def block(r, carry):
+        filter_grad[aligned(r * LANE, LANE, LANE), :] = columns_in[pl.ds(r, CH, stride=8), :].T
+        return carry
+
+    lax.fori_loop(0, 8, block, 0)
+    for i in range(3):
+        in_grad[:, i * CH : (i + 1) * CH] = sums[i * CH : (i + 1) * CH, :]
+    out_grad[...] = sums[384:512, :]
+    stem_grad[...] = sums[512:544, :]
+
+
 def body(samples, stem_weight, in_weight, filter_param, out_weight, cotangent):
     vmem = pl.BlockSpec(memory_space=pltpu.VMEM)
-    stem_padded = jnp.pad(stem_weight, ((0, CH - stem_weight.shape[0]), (0, 0)))
-    return pl.pallas_call(
+    parts = pl.pallas_call(
         kernel,
         out_shape=(
             jax.ShapeDtypeStruct((FR, CH), F32),
             jax.ShapeDtypeStruct((FR, CH), F32),
-            jax.ShapeDtypeStruct((32, CH), F32),
-            jax.ShapeDtypeStruct((CH, 3 * CH), F32),
-            jax.ShapeDtypeStruct((CH, CH), F32),
+            jax.ShapeDtypeStruct((MEMBERS * PIECE, CH), F32),
         ),
         in_specs=[vmem] * 6,
-        out_specs=(vmem,) * 5,
+        out_specs=(vmem,) * 3,
         scratch_shapes=[
             *[pltpu.VMEM((FR, LANE), F32)] * 21,
             pltpu.VMEM((FR, FR), BF16), pltpu.VMEM((FR, FR), BF16),
@@ -482,9 +511,22 @@
             pltpu.SemaphoreType.DMA((6,)), pltpu.SemaphoreType.DMA((6,)),
             pltpu.SemaphoreType.DMA, pltpu.SemaphoreType.DMA,
             pltpu.SemaphoreType.DMA((3,)), pltpu.SemaphoreType.DMA((3,)),
+            pltpu.SemaphoreType.REGULAR,
         ],
-        compiler_params=pltpu.CompilerParams(has_side_effects=True, vmem_limit_bytes=60 * 2**20),
-    )(samples.reshape(LANE, LANE), stem_padded, in_weight, filter_param, out_weight, cotangent)
+        compiler_params=pltpu.CompilerParams(collective_id=0, has_side_effects=True, vmem_limit_bytes=60 * 2**20),
+    )(samples.reshape(LANE, LANE), stem_weight, in_weight, filter_param, out_weight, cotangent)
+    return pl.pallas_call(
+        finish,
+        out_shape=(
+            jax.ShapeDtypeStruct((FR, CH), F32),
+            jax.ShapeDtypeStruct((FR, CH), F32),
+            jax.ShapeDtypeStruct((32, CH), F32),
+            jax.ShapeDtypeStruct((CH, 3 * CH), F32),
+            jax.ShapeDtypeStruct((CH, CH), F32),
+        ),
+        in_specs=[vmem] * 3,
+        out_specs=(vmem,) * 5,
+    )(*parts)
 
 
 def solution(mesh):

time: 129 us -> 125 us (0.969)
  local copies, waits for them, and re-layouts: 6.18 us -> 0 us
  Pallas kernels: 122 us -> 125 us
    unnamed x13 -> x0, local copies, waits for them, and re-layouts: 4.83 us -> none
    pallas_call x0 -> x1, Pallas kernels: none -> 3.11 us  [body(): pl.pallas_call(finish, out_shape=(jax.ShapeDtypeStruct((FR, CH), F32), ja...]
    pad x1 -> x0, local copies, waits for them, and re-layouts: 1.35 us -> none  [body(): stem_padded = jnp.pad(stem_weight, ((0, CH - stem_weight.shape[0]), (0, 0)))]
where the time goes in v2:
time: 125 us
  Pallas kernels  125 us (100%)
    pallas_call x1, Pallas kernels, body(): pl.pallas_call(kernel, out_shape=(jax.ShapeDtypeStruct((FR, CH), F32), ja...  122 us
    pallas_call x1, Pallas kernels, body(): pl.pallas_call(finish, out_shape=(jax.ShapeDtypeStruct((FR, CH), F32), ja...  3.11 us

profile of v2, /device:TPU:1, one launch (start us, length us, event | category | flops | bytes accessed | tf_op | source)
XLA Modules:
  0.0 125.3 jit_solution(11269646008764393521)
XLA Ops:
  0.6 121.5 %shard_map.101 = (f32[1024,128]{1,0:T(8,128)}, f32[1024,128]{1,0:T(8,128)}, f32[640,128]{1,0:T(8,128)}) custom-call(f32[128,128]{1,0:T(8,128)} %bitcast.1, f32[32,128]{1,0:T(8,128)} %stem_w.1, f32[128,384]{1,0:T(8,128)} %in_w.1, f32[1024,128]{1,0:T(8,128)} %filt.1, f32[128,128]{1,0:T(8,128)} %out_w.1, f32[1024,128]{1,0:T(8,128)} %cot.1), custom_call_target="tpu_custom_call" | custom-call | tf_op jit(solution)/shard_map/pallas_call | solution.py:482
  122.1 3.1 %shard_map.102 = (f32[1024,128]{1,0:T(8,128)}, f32[1024,128]{1,0:T(8,128)}, f32[32,128]{1,0:T(8,128)}, f32[128,384]{1,0:T(8,128)}, f32[128,128]{1,0:T(8,128)}) custom-call(f32[1024,128]{1,0:T(8,128)} %get-tuple-element.8.rows_in, f32[1024,128]{1,0:T(8,128)} %get-tuple-element.9.columns_in, f32[640,128]{1,0:T(8,128)} %get-tuple-element.10.sums), custom_call_target="tpu_custom_call" | custom-call | tf_op jit(solution)/shard_map/pallas_call | solution.py:518

commit v3 on v2

--- a/solution.py
+++ b/solution.py
@@ -18,7 +18,11 @@
 HALF = 131072
 ROWS = 528
 CUT = 176
-PIECE = 40
+PIECE = 24
+OWNERS = 23
+PLANE = 32
+SLABS = 8
+CHUNKS = (64, 96, 127)
 MEMBERS = 16
 
 COS_TERMS = [(-1.0) ** i / math.factorial(2 * i) for i in range(9)]
@@ -90,7 +94,7 @@
     def tile(k):
         return aligned(k * 8, 8)
 
-    def scatter(src, dst, unit, slot, own, target):
+    def scatter_some(src, dst, unit, slot, own, target, begin, end):
         def one(i, carry):
             k = (own + 1 + i) % CH
             pltpu.make_async_remote_copy(
@@ -99,7 +103,10 @@
             ).start()
             return carry
 
-        lax.fori_loop(0, CH - 1, one, 0)
+        lax.fori_loop(begin, end, one, 0)
+
+    def scatter(src, dst, unit, slot, own, target, begin=0):
+        scatter_some(src, dst, unit, slot, own, target, begin, CH - 1)
 
         @pl.when(own_half)
         def _():
@@ -134,8 +141,11 @@
     def scatter_in(unit):
         scatter(sbuf[unit], rbuf[unit], unit, place, chip, to_chip)
 
-    def scatter_out(unit):
-        scatter(hbuf[unit], obuf[unit], 3 + unit, chip, place, to_frames)
+    def scatter_out(unit, begin=0):
+        scatter(hbuf[unit], obuf[unit], 3 + unit, chip, place, to_frames, begin)
+
+    def scatter_out_some(unit, begin, end):
+        scatter_some(hbuf[unit], obuf[unit], 3 + unit, chip, place, to_frames, begin, end)
 
     z, x_lo = row // 4, (row // 2) % 2
     first, second_place = z * 2 + core, x_lo * 8 + col
@@ -227,7 +237,6 @@
         return carry
 
     lax.fori_loop(0, MEMBERS - 1, confirm, 0)
-    make_tables()
     pl.semaphore_wait(known, MEMBERS - 1)
 
     @pl.when(dev > 0)
@@ -286,6 +295,7 @@
 
     lax.fori_loop(0, 8, grad_block, 0)
     scatter_in(2)
+    make_tables()
 
     odd = (1 - 2 * (iota((FR, LANE), 0) % 2)).astype(F32)
 
@@ -352,7 +362,6 @@
         exchange(cbuf[unit], 3 + unit)
         exchanged(3 + unit)
         hbuf[unit][...] = xbuf[3 + unit][...] + sign * cbuf[unit][...]
-        scatter_out(unit)
 
     def times(a, b, here):
         x, y = spec[a, here, :], spec[b, here, :]
@@ -376,9 +385,12 @@
     transform(0)
     transform(1)
     inverse(0, plain(0, 1))
+    scatter_out(0)
     transform(2)
     inverse(1, conjugate(0, 2))
+    scatter_out(1)
     inverse(2, conjugate(1, 2))
+    scatter_out_some(2, 0, CHUNKS[0])
 
     gsum[...] = jnp.zeros_like(gsum)
 
@@ -423,26 +435,72 @@
 
     lax.fori_loop(0, 8, back_block, 0)
 
-    def share(step, src, dst, own_place, target):
-        def one(i, carry):
-            m = (own_place + 1 + i) % MEMBERS
-            pltpu.make_async_remote_copy(
-                src(m), dst.at[own_place], rsend.at[step], rrecv.at[step],
-                device_id=target(m), device_id_type=MESH,
-            ).start()
-            return carry
-
-        lax.fori_loop(0, MEMBERS - 1, one, 0)
-        pltpu.make_async_copy(src(own_place), dst.at[own_place], rrecv.at[step]).start()
+    in_plane = (x_lo * 8 + col) * 2 + core
+    owner = in_plane < OWNERS
+
+    def plane_device(m):
+        return (z * 4 + (m // 16) * 2 + m % 2, (m // 2) % 8)
+
+    def slab_device(m):
+        return (m * 4 + row % 4, col)
+
+    def give(step, src, dst, target):
+        pltpu.make_async_remote_copy(
+            src, dst, rsend.at[step], rrecv.at[step], device_id=target, device_id_type=MESH
+        ).start()
+
+    def keep(step, src, dst):
+        pltpu.make_async_copy(src, dst, rrecv.at[step]).start()
+
+    def came(step, dst):
         pltpu.make_async_copy(dst, dst, rrecv.at[step]).wait()
 
-    share(0, lambda m: gsum.at[aligned(m * PIECE, PIECE)], rs_in, first, in_first)
-    red[...] = jnp.sum(rs_in[...], axis=0)
-    share(1, lambda m: red, ag_in, second_place, in_second)
-    tot[...] = jnp.sum(ag_in[...], axis=0) * (2.0 ** -9)
-    share(2, lambda m: tot, fin, first, in_first)
-
-    for m in range(MEMBERS):
+    def give_piece(i, carry):
+        m = (in_plane + i) % OWNERS
+        src = gsum.at[aligned(m * PIECE, PIECE)]
+
+        @pl.when(m == in_plane)
+        def _():
+            keep(0, src, rs_in.at[in_plane])
+
+        @pl.when(m != in_plane)
+        def _():
+            give(0, src, rs_in.at[in_plane], plane_device(m))
+
+        return carry
+
+    lax.fori_loop(0, OWNERS, give_piece, 0)
+    scatter_out_some(2, CHUNKS[0], CHUNKS[1])
+
+    @pl.when(owner)
+    def _():
+        came(0, rs_in)
+        red[...] = jnp.sum(rs_in[...], axis=0)
+
+        def give_slab(i, carry):
+            give(1, red, ag_in.at[z], slab_device((z + 1 + i) % SLABS))
+            return carry
+
+        lax.fori_loop(0, SLABS - 1, give_slab, 0)
+        keep(1, red, ag_in.at[z])
+
+    scatter_out_some(2, CHUNKS[1], CHUNKS[2])
+
+    @pl.when(owner)
+    def _():
+        came(1, ag_in)
+        tot[...] = jnp.sum(ag_in[...], axis=0) * (2.0 ** -9)
+
+        def give_total(i, carry):
+            give(2, tot, fin.at[in_plane], plane_device((in_plane + 1 + i) % PLANE))
+            return carry
+
+        lax.fori_loop(0, PLANE - 1, give_total, 0)
+        keep(2, tot, fin.at[in_plane])
+
+    scatter_out(2, CHUNKS[2])
+    came(2, fin)
+    for m in range(OWNERS):
         sums[m * PIECE : (m + 1) * PIECE, :] = fin[m]
 
     arrived(obuf[2], 5)
@@ -454,9 +512,18 @@
         sent(hbuf[unit], 3 + unit)
         pltpu.make_async_copy(rbuf[unit], rbuf[unit], xsend.at[unit]).wait()
         pltpu.make_async_copy(cbuf[unit], cbuf[unit], xsend.at[3 + unit]).wait()
-    for step in range(3):
-        part = fin.at[pl.ds(0, MEMBERS - 1)]
-        pltpu.make_async_copy(part, part, rsend.at[step]).wait()
+    def left(step, ref):
+        pltpu.make_async_copy(ref, ref, rsend.at[step]).wait()
+
+    @pl.when(owner)
+    def _():
+        left(0, rs_in.at[pl.ds(0, OWNERS - 1)])
+        left(1, ag_in.at[pl.ds(0, SLABS - 1)])
+        left(2, rs_in.at[pl.ds(0, PLANE - 1)])
+
+    @pl.when(jnp.logical_not(owner))
+    def _():
+        left(0, rs_in.at[pl.ds(0, OWNERS)])
 
     @pl.when(dev > 0)
     def _():
@@ -484,7 +551,7 @@
         out_shape=(
             jax.ShapeDtypeStruct((FR, CH), F32),
             jax.ShapeDtypeStruct((FR, CH), F32),
-            jax.ShapeDtypeStruct((MEMBERS * PIECE, CH), F32),
+            jax.ShapeDtypeStruct((OWNERS * PIECE, CH), F32),
         ),
         in_specs=[vmem] * 6,
         out_specs=(vmem,) * 3,
@@ -504,9 +571,9 @@
             pltpu.VMEM((CH, CH), BF16), pltpu.VMEM((CH, CH), BF16),
             pltpu.VMEM((CH, 3 * CH), BF16), pltpu.VMEM((CH, 3 * CH), BF16),
             pltpu.VMEM((CH, CH), BF16), pltpu.VMEM((CH, CH), BF16),
-            pltpu.VMEM((MEMBERS * PIECE, LANE), F32), pltpu.VMEM((MEMBERS, PIECE, LANE), F32),
-            pltpu.VMEM((PIECE, LANE), F32), pltpu.VMEM((MEMBERS, PIECE, LANE), F32),
-            pltpu.VMEM((PIECE, LANE), F32), pltpu.VMEM((MEMBERS, PIECE, LANE), F32),
+            pltpu.VMEM((OWNERS * PIECE, LANE), F32), pltpu.VMEM((PLANE, PIECE, LANE), F32),
+            pltpu.VMEM((PIECE, LANE), F32), pltpu.VMEM((SLABS, PIECE, LANE), F32),
+            pltpu.VMEM((PIECE, LANE), F32), pltpu.VMEM((OWNERS, PIECE, LANE), F32),
             pltpu.SemaphoreType.DMA((6,)), pltpu.SemaphoreType.DMA((6,)),
             pltpu.SemaphoreType.DMA((6,)), pltpu.SemaphoreType.DMA((6,)),
             pltpu.SemaphoreType.DMA, pltpu.SemaphoreType.DMA,

time: 125 us -> 115 us (0.920)
  Pallas kernels: 125 us -> 114 us
    pallas_call x1, Pallas kernels: 122 us -> 111 us  [body(): pl.pallas_call(kernel, out_shape=(jax.ShapeDtypeStruct((FR, CH), F32), ja...]
where the time goes in v3:
time: 115 us
  Pallas kernels  114 us (99%)
    pallas_call x1, Pallas kernels, body(): pl.pallas_call(kernel, out_shape=(jax.ShapeDtypeStruct((FR, CH), F32), ja...  111 us
    pallas_call x1, Pallas kernels, body(): pl.pallas_call(finish, out_shape=(jax.ShapeDtypeStruct((FR, CH), F32), ja...  3.1 us

profile of v3, /device:TPU:1, one launch (start us, length us, event | category | flops | bytes accessed | tf_op | source)
XLA Modules:
  0.0 114.8 jit_solution(10729773109109260906)
XLA Ops:
  0.6 111.0 %shard_map.101 = (f32[1024,128]{1,0:T(8,128)}, f32[1024,128]{1,0:T(8,128)}, f32[552,128]{1,0:T(8,128)}) custom-call(f32[128,128]{1,0:T(8,128)} %bitcast.1, f32[32,128]{1,0:T(8,128)} %stem_w.1, f32[128,384]{1,0:T(8,128)} %in_w.1, f32[1024,128]{1,0:T(8,128)} %filt.1, f32[128,128]{1,0:T(8,128)} %out_w.1, f32[1024,128]{1,0:T(8,128)} %cot.1), custom_call_target="tpu_custom_call" | custom-call | tf_op jit(solution)/shard_map/pallas_call | solution.py:549
  111.7 3.1 %shard_map.102 = (f32[1024,128]{1,0:T(8,128)}, f32[1024,128]{1,0:T(8,128)}, f32[32,128]{1,0:T(8,128)}, f32[128,384]{1,0:T(8,128)}, f32[128,128]{1,0:T(8,128)}) custom-call(f32[1024,128]{1,0:T(8,128)} %get-tuple-element.8.rows_in, f32[1024,128]{1,0:T(8,128)} %get-tuple-element.9.columns_in, f32[552,128]{1,0:T(8,128)} %get-tuple-element.10.sums), custom_call_target="tpu_custom_call" | custom-call | tf_op jit(solution)/shard_map/pallas_call | solution.py:585
